TPU v7x, 32 devices: a whole 2x2x4 slice. The times are simulated.
32 devices in a mesh: expert: 8 (over z, y), mirror: 4 (over x, core).
Axes of the slice: x: 2, y: 2, z: 4, core: 2. Of those that a mesh axis runs over, the one named last changes fastest.
Arguments:
- out_grad: bfloat16 [8, 4, 2, 96, 2048], P('expert', 'mirror'), may hold values from -6 to 6
- gate_prob: float32 [8, 4, 2, 96], P('expert', 'mirror'), may hold values from 0.1 to 1
- dest_expert: int32 [8, 4, 2, 96], P('expert', 'mirror'), may hold values from 0 to 7, as said below
- dest_slot: int32 [8, 4, 2, 96], P('expert', 'mirror'), may hold values from 0 to 31, as said below
- x_saved: bfloat16 [8, 4, 2, 256, 2048], P('expert', 'mirror'), may hold values from -6 to 6
- w_gate_up: bfloat16 [8, 2048, 512], P('expert', 'mirror'), may hold values from -0.125 to 0.125
- w_down: bfloat16 [8, 256, 2048], P('expert', 'mirror'), may hold values from -0.375 to 0.375
Outputs:
- in_grad: bfloat16 [8, 4, 2, 96, 2048], P('expert', 'mirror')
- grad_gate_up: bfloat16 [8, 2048, 512], P('expert', 'mirror')
- grad_down: bfloat16 [8, 256, 2048], P('expert', 'mirror')
Inputs may be any that keep to these rules, and one draw needn't show every extreme that they name: `dest_expert`: rows of one device in one microbatch name no expert more than 32 times. `dest_slot`: rows of one device in one microbatch that name the same expert have different slots.
All inputs are finite; a program needn't handle non-finite values.
Results may differ from a plain program's by a relative error of at most 0.0095.
Values may be sent and summed in bfloat16 or wider, within the bound.
No kernel may reach another device: no remote copies, remote signals or barrier semaphores. Data moves between devices by JAX's collectives and lax.ppermute only.
A program may use at most 64 MiB of HBM per device.

v0:
```python
import jax
import jax.numpy as jnp
from jax import lax
from jax.sharding import PartitionSpec as P


def silu_parts(values):
    sigmoid_vals = jax.nn.sigmoid(values)
    return (values * sigmoid_vals, sigmoid_vals * (1.0 + values * (1.0 - sigmoid_vals)))


def contract_last(left_side, right_side):
    return lax.dot_general(
        left_side, right_side, (((1,), (1,)), ((), ())), preferred_element_type=jnp.float32
    )


def per_device(out_grad, gate_prob, dest_expert, dest_slot, x_saved, w_gate_up, w_down):
    n_expert = lax.axis_size("expert")
    micro_count = x_saved.shape[2]
    capacity = x_saved.shape[3]
    model_width = x_saved.shape[4]
    peer_slots = capacity // n_expert
    hidden_units = w_gate_up.shape[2] // 2
    weighted = (out_grad[0, 0].astype(jnp.float32) * gate_prob[0, 0][..., None]).astype(
        jnp.bfloat16
    )
    position = dest_expert[0, 0] * peer_slots + dest_slot[0, 0]
    slot_ids = jnp.arange(capacity, dtype=jnp.int32)
    placing = (position[:, None, :] == slot_ids[None, :, None]).astype(jnp.bfloat16)
    outgoing = jnp.einsum(
        "bpr,brd->bpd", placing, weighted, preferred_element_type=jnp.float32
    ).astype(jnp.bfloat16)
    outgoing = outgoing.reshape(micro_count, n_expert, peer_slots, model_width)
    saved_inputs = x_saved[0, 0]
    full_gu, full_down = (
        lax.all_gather(w_gate_up, "mirror", axis=1, tiled=True),
        lax.all_gather(w_down, "mirror", axis=1, tiled=True),
    )
    full_gu = full_gu[0]
    full_down = full_down[0]
    arrived = lax.all_to_all(outgoing, "expert", split_axis=1, concat_axis=1, tiled=True)
    grads_flat = arrived.reshape(micro_count * capacity, model_width)
    gate_up = jnp.dot(
        saved_inputs.reshape(micro_count * capacity, model_width),
        full_gu,
        preferred_element_type=jnp.float32,
    )
    gate_part = gate_up[:, :hidden_units]
    up_part = gate_up[:, hidden_units:]
    activation, slope_term = silu_parts(gate_part)
    hidden = (activation * up_part).astype(jnp.bfloat16)
    unit_grad = contract_last(grads_flat, full_down)
    gu_grad = jnp.concatenate(
        [unit_grad * up_part * slope_term, unit_grad * activation], axis=1
    ).astype(jnp.bfloat16)
    input_rows = contract_last(gu_grad, full_gu).astype(jnp.bfloat16)
    input_rows, hidden, gu_grad = (input_rows, hidden, gu_grad)
    returned = lax.all_to_all(
        input_rows.reshape(micro_count, n_expert, peer_slots, model_width),
        "expert",
        split_axis=1,
        concat_axis=1,
        tiled=True,
    )
    back_rows = returned.reshape(micro_count, capacity, model_width)
    in_rows = jnp.einsum(
        "bpr,bpd->brd", placing, back_rows, preferred_element_type=jnp.float32
    ).astype(jnp.bfloat16)
    flat_inputs = saved_inputs.reshape(micro_count * capacity, model_width)
    term_gu = jnp.einsum("sd,sf->df", flat_inputs, gu_grad, preferred_element_type=jnp.float32)
    term_down = jnp.einsum("sf,sd->fd", hidden, grads_flat, preferred_element_type=jnp.float32)
    share_gu, share_down = (
        lax.psum_scatter(
            term_gu.astype(jnp.bfloat16), "mirror", scatter_dimension=0, tiled=True
        ).astype(jnp.float32),
        lax.psum_scatter(
            term_down.astype(jnp.bfloat16), "mirror", scatter_dimension=0, tiled=True
        ).astype(jnp.float32),
    )
    return (
        in_rows[None, None],
        share_gu.astype(jnp.bfloat16)[None],
        share_down.astype(jnp.bfloat16)[None],
    )


def solution(mesh):
    in_specs = (
        P("expert", "mirror", None, None, None),
        P("expert", "mirror", None, None),
        P("expert", "mirror", None, None),
        P("expert", "mirror", None, None),
        P("expert", "mirror", None, None, None),
        P("expert", "mirror", None),
        P("expert", "mirror", None),
    )
    out_specs = (
        P("expert", "mirror", None, None, None),
        P("expert", "mirror", None),
        P("expert", "mirror", None),
    )
    return jax.shard_map(
        per_device, mesh=mesh, in_specs=in_specs, out_specs=out_specs, check_vma=False
    )
```

profile of v0, /device:TPU:0, one launch (start us, length us, event | category | flops | bytes accessed | tf_op | source)
XLA Modules:
  0.0 145.3 jit_solution(14282525532056262825)
XLA Ops:
  7.2 0.0 all-gather.5.cloned.1.call-start
  7.2 0.7 all-gather.5.cloned.1.call-update
  7.9 0.7 add_bitcast_fusion
  8.6 2.0 %convolution_convert_fusion = bf16[2,256,2048]{2,1,0:T(8,128)(2,1)S(1)} fusion(bf16[1,1,2,96,2048]{4,3,2,1,0:T(8,128)(2,1)} %param.7, f32[2,96]{1,0:T(2,128)} %bitcast.43, s32[2,96]{1,0:T(2,128)S(1)} %add_bitcast_fusion), kind=kOutput, calls=%fused_computation | convolution fusion | flops 203603968 | bytes 2885120 | tf_op jit(solution)/shard_map/bpr,brd->bpd/dot_general | solution.py:31
  10.6 1.4 copy.15
  12.0 7.3 %all-to-all-start = ((bf16[2,8,32,2048]{3,2,0,1:T(8,128)(2,1)}), bf16[2,8,32,2048]{3,2,0,1:T(8,128)(2,1)}, u32[]{:S(2)}, u32[]{:S(2)}) async-start(bf16[2,8,32,2048]{3,2,0,1:T(8,128)(2,1)} %copy.15), calls=%async_computation | async-start | bytes 4194304 | tf_op jit(solution)/shard_map/all_to_all | solution.py:42
  19.4 0.7 all-gather.3.cloned.1.call-update
  20.1 0.0 reduce-scatter.3.cloned.1.call-start
  20.1 14.7 %all-gather.5.cloned.1.call-done = bf16[1,2048,512]{2,1,0:T(8,128)(2,1)} async-done(((bf16[1,512,512]{2,1,0:T(8,128)(2,1)}), bf16[1,2048,512]{2,1,0:T(8,128)(2,1)}) %all-gather.5.cloned.1.call-update) | async-done | bytes 2097168 | tf_op jit(solution)/shard_map/all_gather | solution.py:37
  34.9 2.9 %fusion.3 = f32[512,512]{0,1:T(8,128)S(1)} fusion(bf16[512,2048]{1,0:T(8,128)(2,1)S(1)} %bitcast.35, bf16[1,2048,512]{2,1,0:T(8,128)(2,1)} %all-gather.5.cloned.1.call-done), kind=kOutput, calls=%fused_computation.8 | convolution fusion | flops 1073741824 | bytes 5242880 | tf_op jit(solution)/shard_map/dot_general | solution.py:44
  37.8 29.9 %all-to-all-done = bf16[2,8,32,2048]{3,2,0,1:T(8,128)(2,1)} async-done(((bf16[2,8,32,2048]{3,2,0,1:T(8,128)(2,1)}), bf16[2,8,32,2048]{3,2,0,1:T(8,128)(2,1)}, u32[]{:S(2)}, u32[]{:S(2)}) %all-to-all-start) | async-done | bytes 2097184 | tf_op jit(solution)/shard_map/all_to_all | solution.py:42
  67.7 3.1 %copy.16 = bf16[2,8,32,2048]{3,2,1,0:T(8,128)(2,1)} copy(bf16[2,8,32,2048]{3,2,0,1:T(8,128)(2,1)} %all-to-all-done) | data formatting | bytes 4194304 | tf_op jit(solution)/shard_map/all_to_all | solution.py:42
  70.8 2.7 %multiply_convert_fusion.2 = (bf16[512,256]{0,1:T(8,128)(2,1)S(1)}, bf16[512,256]{0,1:T(8,128)(2,1)S(1)}) fusion(f32[512,512]{0,1:T(8,128)S(1)} %fusion.3, bf16[512,2048]{1,0:T(8,128)(2,1)} %bitcast.39, bf16[1,256,2048]{2,1,0:T(8,128)(2,1)} %all-gather.3.cloned.1.call-done), kind=kOutput, calls=%fused_computation.19 | convolution fusion | flops 538574848 | bytes 4718592 | tf_op jit(solution)/shard_map/dot_general | solution.py:13
  73.6 0.7 copy-done.1
  74.3 2.6 %fusion = bf16[2048,512]{0,1:T(8,128)(2,1)} fusion(bf16[512,2048]{1,0:T(8,128)(2,1)S(1)} %bitcast.36, bf16[512,256]{0,1:T(8,128)(2,1)S(1)} %get-tuple-element.13, bf16[512,256]{0,1:T(8,128)(2,1)S(1)} %get-tuple-element.12), kind=kOutput, calls=%fused_computation.3 | convolution fusion | flops 1075838976 | bytes 4718592 | tf_op jit(solution)/shard_map/sd,sf->df/dot_general | solution.py:71
  76.9 3.0 %convolution_convert_fusion.2 = bf16[512,2048]{1,0:T(8,128)(2,1)S(1)} fusion(bf16[1,2048,512]{2,1,0:T(8,128)(2,1)} %all-gather.5.cloned.1.call-done, bf16[512,256]{0,1:T(8,128)(2,1)} %copy-done.1, bf16[512,256]{0,1:T(8,128)(2,1)S(1)} %get-tuple-element.12), kind=kOutput, calls=%fused_computation.2 | convolution fusion | flops 1075838976 | bytes 4718592 | tf_op jit(solution)/shard_map/dot_general | solution.py:13
  79.9 1.5 %copy.17 = bf16[2,8,32,2048]{3,2,0,1:T(8,128)(2,1)} copy(bf16[2,8,32,2048]{3,2,1,0:T(8,128)(2,1)S(1)} %bitcast.41) | data formatting | bytes 4194304 | tf_op jit(solution)/shard_map/reshape | solution.py:60
  81.4 4.4 %all-to-all-start.1 = ((bf16[2,8,32,2048]{3,2,0,1:T(8,128)(2,1)}), bf16[2,8,32,2048]{3,2,0,1:T(8,128)(2,1)}, u32[]{:S(2)}, u32[]{:S(2)}) async-start(bf16[2,8,32,2048]{3,2,0,1:T(8,128)(2,1)} %copy.17), calls=%async_computation.1 | async-start | bytes 4194304 | tf_op jit(solution)/shard_map/all_to_all | solution.py:59
  85.8 0.0 reduce-scatter.5.cloned.1.call-start
  85.9 3.4 %convolution_convert_fusion.3 = bf16[256,2048]{1,0:T(8,128)(2,1)} fusion(bf16[512,2048]{1,0:T(8,128)(2,1)} %bitcast.40, f32[512,512]{0,1:T(8,128)S(1)} %fusion.3), kind=kOutput, calls=%fused_computation.4 | convolution fusion | flops 538181632 | bytes 4194304 | tf_op jit(solution)/shard_map/sf,sd->fd/dot_general | solution.py:72
  89.3 44.3 %all-to-all-done.1 = bf16[2,8,32,2048]{3,2,0,1:T(8,128)(2,1)} async-done(((bf16[2,8,32,2048]{3,2,0,1:T(8,128)(2,1)}), bf16[2,8,32,2048]{3,2,0,1:T(8,128)(2,1)}, u32[]{:S(2)}, u32[]{:S(2)}) %all-to-all-start.1) | async-done | bytes 2097184 | tf_op jit(solution)/shard_map/all_to_all | solution.py:59
  133.6 1.7 %copy.18 = bf16[2,8,32,2048]{3,2,1,0:T(8,128)(2,1)S(1)} copy(bf16[2,8,32,2048]{3,2,0,1:T(8,128)(2,1)} %all-to-all-done.1) | data formatting | bytes 4194304 | tf_op jit(solution)/shard_map/all_to_all | solution.py:59
  135.3 1.4 fusion.1
  136.7 2.0 %copy.19 = bf16[1,512,512]{2,1,0:T(8,128)(2,1)} copy(bf16[1,512,512]{1,2,0:T(8,128)(2,1)} %bitcast.42) | data formatting | bytes 1048576
  (9 shorter events, 0.1 us)
Async XLA Ops:
  7.2 27.7 %copy-start = (bf16[1,1,2,256,2048]{4,3,2,1,0:T(8,128)(2,1)S(1)}, bf16[1,1,2,256,2048]{4,3,2,1,0:T(8,128)(2,1)}, u32[]{:S(2)}) copy-start(bf16[1,1,2,256,2048]{4,3,2,1,0:T(8,128)(2,1)} %param.11) | copy-start | bytes 6291460
  7.2 27.7 %all-gather.5.cloned.1.call-start = ((), (), s32[]{:S(2)}) async-start(), calls=%async_computation.5 | async-start | bytes 2621440 | tf_op jit(solution)/shard_map/all_gather | solution.py:37
  12.0 55.7 %all-to-all-start = ((bf16[2,8,32,2048]{3,2,0,1:T(8,128)(2,1)}), bf16[2,8,32,2048]{3,2,0,1:T(8,128)(2,1)}, u32[]{:S(2)}, u32[]{:S(2)}) async-start(bf16[2,8,32,2048]{3,2,0,1:T(8,128)(2,1)} %copy.15), calls=%async_computation | async-start | bytes 4194304 | tf_op jit(solution)/shard_map/all_to_all | solution.py:42
  19.3 51.5 %all-gather.3.cloned.1.call-start = ((), (), s32[]{:S(2)}) async-start(), calls=%async_computation.4 | async-start | bytes 1310720 | tf_op jit(solution)/shard_map/all_gather | solution.py:38
  20.1 116.7 %reduce-scatter.3.cloned.1.call-start = ((), (), s32[]{:S(2)}) async-start(), calls=%async_computation.6 | async-start | bytes 2621440 | tf_op jit(solution)/shard_map/reduce_scatter | solution.py:74
  73.6 0.7 copy-start.1
  81.4 52.2 %all-to-all-start.1 = ((bf16[2,8,32,2048]{3,2,0,1:T(8,128)(2,1)}), bf16[2,8,32,2048]{3,2,0,1:T(8,128)(2,1)}, u32[]{:S(2)}, u32[]{:S(2)}) async-start(bf16[2,8,32,2048]{3,2,0,1:T(8,128)(2,1)} %copy.17), calls=%async_computation.1 | async-start | bytes 4194304 | tf_op jit(solution)/shard_map/all_to_all | solution.py:59
  85.8 53.0 %reduce-scatter.5.cloned.1.call-start = ((), (), s32[]{:S(2)}) async-start(), calls=%async_computation.7 | async-start | bytes 1310720 | tf_op jit(solution)/shard_map/reduce_scatter | solution.py:77
Sparse Core Ops, SparseCore 0:
  9.5 25.2 all-gather.4
  36.4 16.6 all-gather.2
  77.0 30.1 reduce-scatter.2
  110.2 24.7 reduce-scatter.4
where the time goes:
time: 146 us; the launch traced here: 145 us
  waiting for transfers between devices  90.3 us (62%)
  matrix products  18 us (12%)
  between operations  13.8 us (9%)
  starting transfers between devices  11.8 us (8%)
  local copies, waits for them, and re-layouts  10.6 us (7%)
    all_to_all x1, waiting for transfers between devices, per_device(): lax.all_to_all(input_rows.reshape(micro_count, n_expert, peer_slots, mode...  44.3 us
    all_to_all x1, waiting for transfers between devices, per_device(): lax.all_to_all(outgoing, 'expert', split_axis=1, concat_axis=1, tiled=True)  29.9 us
    all_gather x1, waiting for transfers between devices, per_device(): lax.all_gather(w_gate_up, 'mirror', axis=1, tiled=True)  14.7 us
    all_to_all x1, starting transfers between devices, per_device(): lax.all_to_all(outgoing, 'expert', split_axis=1, concat_axis=1, tiled=True)  7.31 us
    dot_general x2, matrix products, contract_last(): lax.dot_general(left_side, right_side, (((1,), (1,)), ((), ())), preferre...  5.74 us
    all_to_all x1, starting transfers between devices, per_device(): lax.all_to_all(input_rows.reshape(micro_count, n_expert, peer_slots, mode...  4.37 us
    dot_general x1, matrix products, per_device(): jnp.einsum('sf,sd->fd', hidden, grads_flat, preferred_element_type=jnp.fl...  3.44 us
    all_to_all x1, local copies, waits for them, and re-layouts, per_device(): lax.all_to_all(outgoing, 'expert', split_axis=1, concat_axis=1, tiled=True)  3.15 us
  transfers between devices with their start and end apart: 6, of which 3 were waited for; matrix products, arithmetic and copies ran while one was open for 16% of the time, Pallas kernels for 0%

commit v1 on v0

v1 whole, which is shorter than its diff:
```python
import jax
import jax.numpy as jnp
from jax import lax
from jax.experimental import pallas as pl
from jax.experimental.pallas import tpu as pltpu
from jax.sharding import PartitionSpec as P


BF16 = jnp.bfloat16
F32 = jnp.float32
VMEM_LIMIT = 12 * 1024 * 1024


def copied_spec(shape):
    zeros = (0,) * len(shape)
    return pl.BlockSpec(tuple(shape), lambda i: zeros)


def resident_spec():
    return pl.BlockSpec(memory_space=pltpu.VMEM)


def call(body, operands, out_shapes, flops=0, scratch=(), in_specs=None, out_specs=None, aliases=None, steps=1, exps=0):
    shapes = [jax.ShapeDtypeStruct(shape, dtype) for shape, dtype in out_shapes]
    moved = sum(v.size * v.dtype.itemsize for v in (*operands, *shapes))
    return pl.pallas_call(
        body,
        grid=(steps,),
        in_specs=in_specs or [resident_spec()] * len(operands),
        out_specs=out_specs or [resident_spec()] * len(shapes),
        out_shape=shapes,
        scratch_shapes=list(scratch),
        input_output_aliases=aliases or {},
        compiler_params=pltpu.CompilerParams(vmem_limit_bytes=VMEM_LIMIT),
        cost_estimate=pl.CostEstimate(flops=flops, bytes_accessed=moved, transcendentals=exps),
    )(*operands)


def dot_nt(left_side, right_side):
    return lax.dot_general(
        left_side, right_side, (((1,), (1,)), ((), ())), preferred_element_type=F32
    )


def dot_tn(left_side, right_side):
    return lax.dot_general(
        left_side, right_side, (((0,), (0,)), ((), ())), preferred_element_type=F32
    )


def silu_parts(values):
    sigmoid_vals = jax.nn.sigmoid(values)
    return (values * sigmoid_vals, sigmoid_vals * (1.0 + values * (1.0 - sigmoid_vals)))


def swap(value, axis, bit):
    size = lax.axis_size(axis)
    return lax.ppermute(value, axis, [(i, i ^ bit) for i in range(size)])


def as_column(row):
    count = row.shape[1]
    down = lax.broadcasted_iota(jnp.int32, (count, count), 0)
    across = lax.broadcasted_iota(jnp.int32, (count, count), 1)
    spread = jnp.broadcast_to(row, (count, count))
    return jnp.sum(jnp.where(down == across, spread, jnp.zeros_like(spread)), axis=1, keepdims=True)


def relative_position(expert_ref, slot_ref, b, peer_slots, relative):
    expert_row = expert_ref[b : b + 1, :]
    if relative:
        expert_row = expert_row ^ lax.axis_index("expert")
    return expert_row * peer_slots + slot_ref[b : b + 1, :]


STEP = 512


def place_rows(out_grad, gate_prob, dest_expert, dest_slot, b, n_expert, peer_slots, relative, after):
    rows, width = out_grad.shape[1:]
    capacity = n_expert * peer_slots
    operands = [out_grad, gate_prob, dest_expert, dest_slot]
    in_specs = [pl.BlockSpec((1, rows, width), lambda i: (b, 0, 0))]
    in_specs += [copied_spec(v.shape) for v in operands[1:]]
    if after is not None:
        operands.append(after)
        in_specs.append(pl.BlockSpec(memory_space=pl.ANY))

    def body(grad_ref, prob_ref, expert_ref, slot_ref, *refs):
        out_refs = refs[-count:]
        position = relative_position(expert_ref, slot_ref, b, peer_slots, relative)
        slot_ids = lax.broadcasted_iota(jnp.int32, (capacity, rows), 0)
        placing = jnp.where(slot_ids == position, 1.0, 0.0).astype(BF16)
        prob = as_column(prob_ref[b : b + 1, :])
        for start in range(0, width, STEP):
            columns = slice(start, start + STEP)
            weighted = (grad_ref[0, :, columns].astype(F32) * prob).astype(BF16)
            slots = jnp.dot(placing, weighted, preferred_element_type=F32).astype(BF16)
            if relative:
                for k in range(n_expert):
                    out_refs[k][:, columns] = slots[k * peer_slots : (k + 1) * peer_slots]
            else:
                out_refs[0][:, columns] = slots

    count, block_rows = (n_expert, peer_slots) if relative else (1, capacity)
    return call(
        body,
        operands,
        [((block_rows, width), BF16)] * count,
        flops=2 * capacity * rows * width,
        in_specs=in_specs,
    )


def prepare(pieces_gu, pieces_down, saved):
    rows_gu, both = pieces_gu[0].shape
    rows_down, width = pieces_down[0].shape
    count = len(pieces_gu)
    slots = saved.shape[0]

    def body(*refs):
        mine = lax.axis_index("mirror")
        saved_ref = refs[2 * count]
        gu_ref, down_ref, gate_up_ref = refs[2 * count + 1 :]
        total = None
        for j in range(count):
            at = pl.ds(pl.multiple_of((mine ^ j) * rows_gu, rows_gu), rows_gu)
            gu_ref[at, :] = refs[j][...]
            term = jnp.dot(saved_ref[:, at], refs[j][...], preferred_element_type=F32)
            total = term if total is None else total + term
            down = pl.ds(pl.multiple_of((mine ^ j) * rows_down, rows_down), rows_down)
            down_ref[down, :] = refs[count + j][...]
        gate_up_ref[...] = total

    return call(
        body,
        [*pieces_gu, *pieces_down, saved],
        [((count * rows_gu, both), BF16), ((count * rows_down, width), BF16), ((slots, both), F32)],
        flops=2 * slots * width * both,
    )


def expert_rows(arrived, gate_up, full_gu, full_down, b, n_expert, relative):
    both = gate_up.shape[1]
    hidden_units = both // 2
    width = full_gu.shape[0]
    count = len(arrived)
    peer_slots = arrived[0].shape[0] if relative else arrived[0].shape[0] // n_expert
    capacity = n_expert * peer_slots

    def body(*refs):
        blocks = refs[:count]
        gate_up_ref, gu_ref, down_ref = refs[count : count + 3]
        rows_refs = refs[count + 3 : 2 * count + 3]
        grad_ref, hidden_ref = refs[2 * count + 3 : 2 * count + 5]
        if relative:
            slots_ref, stage = refs[2 * count + 5 :]
            me = lax.axis_index("expert")
            spots = [
                pl.ds(pl.multiple_of((me ^ k) * peer_slots, peer_slots), peer_slots)
                for k in range(n_expert)
            ]
            for k in range(n_expert):
                slots_ref[spots[k], :] = blocks[k][...]
            unit_grad = dot_nt(slots_ref[...], down_ref[...])
        else:
            unit_grad = dot_nt(blocks[0][...], down_ref[...])
        mine = slice(b * capacity, (b + 1) * capacity)
        gate_part = gate_up_ref[mine, :hidden_units]
        up_part = gate_up_ref[mine, hidden_units:]
        activation, slope_term = silu_parts(gate_part)
        hidden_ref[...] = (activation * up_part).astype(BF16)
        grad_ref[:, :hidden_units] = (unit_grad * up_part * slope_term).astype(BF16)
        grad_ref[:, hidden_units:] = (unit_grad * activation).astype(BF16)
        for start in range(0, width, STEP):
            rows = dot_nt(grad_ref[...], gu_ref[start : start + STEP, :]).astype(BF16)
            if relative:
                stage[:, start : start + STEP] = rows
            else:
                rows_refs[0][:, start : start + STEP] = rows
        if relative:
            for k in range(n_expert):
                rows_refs[k][...] = stage[spots[k], :]

    out_shapes = [(arrived[0].shape, BF16)] * count
    out_shapes += [((capacity, both), BF16), ((capacity, hidden_units), BF16)]
    if relative:
        out_shapes.append(((capacity, width), BF16))
    operands = [*arrived, gate_up, full_gu, full_down]
    return call(
        body,
        operands,
        out_shapes,
        flops=2 * capacity * width * (both + hidden_units),
        exps=capacity * hidden_units,
        scratch=[pltpu.VMEM((capacity, width), BF16)] if relative else [],
    )


def unplace_rows(back, dest_expert, dest_slot, b, n_expert, relative, rows, previous, micro_count):
    width = back[0].shape[1]
    count = len(back)
    peer_slots = back[0].shape[0] if relative else back[0].shape[0] // n_expert
    capacity = n_expert * peer_slots

    def body(*refs):
        expert_ref, slot_ref = refs[:2]
        blocks = refs[2 : 2 + count]
        out_ref = refs[-2] if relative else refs[-1]
        position = as_column(relative_position(expert_ref, slot_ref, b, peer_slots, relative))
        slot_ids = lax.broadcasted_iota(jnp.int32, (rows, capacity), 1)
        taking = jnp.where(slot_ids == position, 1.0, 0.0).astype(BF16)
        if relative:
            stage = refs[-1]
            for k in range(n_expert):
                stage[k * peer_slots : (k + 1) * peer_slots, :] = blocks[k][...]
        else:
            stage = blocks[0]
        for start in range(0, width, STEP):
            columns = slice(start, start + STEP)
            out_ref[0, :, columns] = jnp.dot(
                taking, stage[:, columns], preferred_element_type=F32
            ).astype(BF16)

    operands = [dest_expert, dest_slot, *back]
    in_specs = [copied_spec(v.shape) for v in operands[:2]] + [resident_spec()] * count
    aliases = {}
    if previous is not None:
        aliases = {len(operands): 0}
        operands.append(previous)
        in_specs.append(pl.BlockSpec(memory_space=pl.ANY))
    return call(
        body,
        operands,
        [((micro_count, rows, width), BF16)],
        flops=2 * capacity * rows * width,
        in_specs=in_specs,
        out_specs=[pl.BlockSpec((1, rows, width), lambda i: (b, 0, 0))],
        scratch=[pltpu.VMEM((capacity, width), BF16)] if relative else [],
        aliases=aliases,
    )[0]


def weight_parts(saved, grads, hidden, slots):
    micro_count = len(grads)
    capacity, both = grads[0].shape
    hidden_units = hidden[0].shape[1]
    width = saved.shape[1]
    rows_gu, rows_down = width // 4, hidden_units // 4
    folds = width // both
    tall = rows_gu + rows_down * folds

    def body(*refs):
        saved_ref = refs[0]
        grad_refs = refs[1 : 1 + micro_count]
        hidden_refs = refs[1 + micro_count : 1 + 2 * micro_count]
        slot_refs = refs[1 + 2 * micro_count : 1 + 3 * micro_count]
        near_ref, ours_ref, down = refs[1 + 3 * micro_count :]
        mine = lax.axis_index("mirror")
        for c in range(folds):
            columns = slice(c * both, (c + 1) * both)
            down[c] = sum(
                dot_tn(hidden_refs[b][...], slot_refs[b][:, columns]) for b in range(micro_count)
            ).astype(BF16)
        for out_ref, place, j in ((near_ref, 0, 1), (near_ref, 1, 3), (ours_ref, 0, 0), (ours_ref, 1, 2)):
            at = pl.ds(pl.multiple_of((mine ^ j) * rows_gu, rows_gu), rows_gu)
            out_ref[place, :rows_gu, :] = sum(
                dot_tn(saved_ref[b * capacity : (b + 1) * capacity, at], grad_refs[b][...])
                for b in range(micro_count)
            ).astype(BF16)
            at = pl.ds(pl.multiple_of((mine ^ j) * rows_down, rows_down), rows_down)
            for c in range(folds):
                base = rows_gu + c * rows_down
                out_ref[place, base : base + rows_down, :] = down[c, at, :]

    return call(
        body,
        [saved, *grads, *hidden, *slots],
        [((2, tall, both), BF16)] * 2,
        flops=2 * micro_count * capacity * width * (both + hidden_units),
        scratch=[pltpu.VMEM((folds, hidden_units, both), BF16)],
    )


def near_sum(ours, near):
    def body(ours_ref, near_ref, out_ref):
        out_ref[...] = (ours_ref[1].astype(F32) + near_ref[1].astype(F32)).astype(BF16)

    return call(body, [ours, near], [(ours.shape[1:], BF16)])[0]


def final_sum(ours, near, far, rows_gu, rows_down):
    both = far.shape[1]
    folds = (far.shape[0] - rows_gu) // rows_down

    def body(ours_ref, near_ref, far_ref, gu_ref, down_ref):
        total = ours_ref[0].astype(F32) + near_ref[0].astype(F32) + far_ref[...].astype(F32)
        total = total.astype(BF16)
        gu_ref[...] = total[:rows_gu]
        for c in range(folds):
            base = rows_gu + c * rows_down
            down_ref[:, c * both : (c + 1) * both] = total[base : base + rows_down]

    shapes = [(rows_gu, both), (rows_down, both * folds)]
    return call(
        body,
        [ours, near, far],
        [(shape, BF16) for shape in shapes],
        out_specs=[copied_spec(shape) for shape in shapes],
    )


def gather_pieces(shards):
    far = [swap(shard, "mirror", 2) for shard in shards]
    near = [swap(shard, "mirror", 1) for shard in shards]
    corner = [swap(piece, "mirror", 1) for piece in far]
    return [list(pieces) for pieces in zip(shards, near, far, corner)]


def per_device(out_grad, gate_prob, dest_expert, dest_slot, x_saved, w_gate_up, w_down):
    n_expert = lax.axis_size("expert")
    micro_count = x_saved.shape[2]
    capacity = x_saved.shape[3]
    width = x_saved.shape[4]
    peer_slots = capacity // n_expert
    rows = out_grad.shape[3]
    small = n_expert <= 16
    permuted = [small and b % 2 == 0 for b in range(micro_count)]
    order = sorted(range(1, n_expert), key=lambda k: -k)

    def exchange(blocks, relative):
        if relative:
            moved = {0: blocks[0]}
            for k in order:
                moved[k] = swap(blocks[k], "expert", k)
            return [moved[k] for k in range(n_expert)]
        value = blocks[0]
        parts = value.reshape(n_expert, peer_slots, width)
        moved = lax.all_to_all(parts, "expert", split_axis=0, concat_axis=0, tiled=True)
        return [moved.reshape(value.shape)]

    grad, prob = out_grad[0, 0], gate_prob[0, 0]
    expert, slot = dest_expert[0, 0], dest_slot[0, 0]
    saved = x_saved[0, 0].reshape(micro_count * capacity, width)
    pieces_gu, pieces_down = gather_pieces([w_gate_up[0], w_down[0]])
    arrived = []
    after = None
    for b in range(micro_count):
        placed = place_rows(grad, prob, expert, slot, b, n_expert, peer_slots, permuted[b], after)
        after = placed[0]
        arrived.append(exchange(placed, permuted[b]))
    full_gu, full_down, gate_up = prepare(pieces_gu, pieces_down, saved)

    hidden_all, gu_all, slot_all, backs = [], [], [], []
    for b in range(micro_count):
        results = expert_rows(arrived[b], gate_up, full_gu, full_down, b, n_expert, permuted[b])
        count = len(arrived[b])
        gu_all.append(results[count])
        hidden_all.append(results[count + 1])
        slot_all.append(results[count + 2] if permuted[b] else arrived[b][0])
        backs.append(exchange(results[:count], permuted[b]))
    near, ours = weight_parts(saved, gu_all, hidden_all, slot_all)
    got_near = swap(near, "mirror", 1)
    pair = near_sum(ours, got_near)
    got_far = swap(pair, "mirror", 2)
    share_gu, share_down = final_sum(ours, got_near, got_far, w_gate_up.shape[1], w_down.shape[1])
    in_rows = None
    for b in range(micro_count):
        in_rows = unplace_rows(
            backs[b], expert, slot, b, n_expert, permuted[b], rows, in_rows, micro_count
        )
    return (in_rows[None, None], share_gu[None], share_down[None])


def solution(mesh):
    in_specs = (
        P("expert", "mirror", None, None, None),
        P("expert", "mirror", None, None),
        P("expert", "mirror", None, None),
        P("expert", "mirror", None, None),
        P("expert", "mirror", None, None, None),
        P("expert", "mirror", None),
        P("expert", "mirror", None),
    )
    out_specs = (
        P("expert", "mirror", None, None, None),
        P("expert", "mirror", None),
        P("expert", "mirror", None),
    )
    return jax.shard_map(
        per_device, mesh=mesh, in_specs=in_specs, out_specs=out_specs, check_vma=False
    )
```

time: 146 us -> 145 us (level)
  the two profiles are of different devices: /device:TPU:0 before, /device:TPU:8 now
where the time goes in v1:
time: 145 us; the launch traced here: 144 us
  waiting for transfers between devices  61 us (42%)
  starting transfers between devices  46.6 us (32%)
  Pallas kernels  19.3 us (13%)
  local copies, waits for them, and re-layouts  16.7 us (12%)
    ppermute x22, waiting for transfers between devices, swap(): return lax.ppermute(value, axis, [(i, i ^ bit) for i in range(size)])  61 us
    ppermute x22, starting transfers between devices, swap(): return lax.ppermute(value, axis, [(i, i ^ bit) for i in range(size)])  34 us
    pallas_call x10, Pallas kernels, call(): pl.pallas_call(body, grid=(steps,), in_specs=in_specs or [resident_spec()...  19.3 us
    unnamed x68, local copies, waits for them, and re-layouts  16.7 us
    all_to_all x2, starting transfers between devices, exchange(): lax.all_to_all(parts, 'expert', split_axis=0, concat_axis=0, tiled=True)  12.6 us
  transfers between devices with their start and end apart: 24, of which 13 were waited for; matrix products, arithmetic and copies ran while one was open for 0% of the time, Pallas kernels for 5%

profile of v1, /device:TPU:8, one launch (start us, length us, event | category | flops | bytes accessed | tf_op | source)
XLA Modules:
  0.0 144.3 jit_solution(7439379019621887286)
XLA Ops:
  7.9 6.3 %all-to-all-start = ((bf16[8,32,2048]{2,1,0:T(8,128)(2,1)}), bf16[8,32,2048]{2,1,0:T(8,128)(2,1)}, u32[]{:S(2)}, u32[]{:S(2)}) async-start(bf16[8,32,2048]{2,1,0:T(8,128)(2,1)} %bitcast.4), calls=%async_computation | async-start | bytes 2097152 | tf_op jit(solution)/shard_map/all_to_all | solution.py:339
  16.2 12.8 %collective-permute-done.1.refs_2_ = bf16[512,512]{1,0:T(8,128)(2,1)S(1)} collective-permute-done((bf16[512,512]{1,0:T(8,128)(2,1)S(1)}, bf16[512,512]{1,0:T(8,128)(2,1)S(1)}, u32[]{:S(2)}, u32[]{:S(2)}) %collective-permute-start.1) | collective-permute-done | bytes 524320 | tf_op jit(solution)/shard_map/ppermute | solution.py:58
  29.0 3.3 %collective-permute-start.10 = (bf16[32,2048]{1,0:T(8,128)(2,1)S(1)}, bf16[32,2048]{1,0:T(8,128)(2,1)S(1)}, u32[]{:S(2)}, u32[]{:S(2)}) collective-permute-start(bf16[32,2048]{1,0:T(8,128)(2,1)S(1)} %get-tuple-element.41), channel_id=1, source_target_pairs={{0,20},{4,16},{8,28},{12,24},{16,4},{20,0},{24,12},{28,8},{1,21},{... | collective-permute-start | bytes 393224 | tf_op jit(solution)/shard_map/ppermute | solution.py:58
  32.9 9.0 %collective-permute-done.10.refs_5_ = bf16[32,2048]{1,0:T(8,128)(2,1)S(1)} collective-permute-done((bf16[32,2048]{1,0:T(8,128)(2,1)S(1)}, bf16[32,2048]{1,0:T(8,128)(2,1)S(1)}, u32[]{:S(2)}, u32[]{:S(2)}) %collective-permute-start.10) | collective-permute-done | bytes 131104 | tf_op jit(solution)/shard_map/ppermute | solution.py:58
  41.9 1.7 %collective-permute-start.11 = (bf16[32,2048]{1,0:T(8,128)(2,1)S(1)}, bf16[32,2048]{1,0:T(8,128)(2,1)S(1)}, u32[]{:S(2)}, u32[]{:S(2)}) collective-permute-start(bf16[32,2048]{1,0:T(8,128)(2,1)S(1)} %get-tuple-element.42), channel_id=1, source_target_pairs={{0,24},{4,28},{8,16},{12,20},{16,8},{20,12},{24,0},{28,4},{1,25},{... | collective-permute-start | bytes 393224 | tf_op jit(solution)/shard_map/ppermute | solution.py:58
  43.7 3.7 %collective-permute-done.11.refs_6_ = bf16[32,2048]{1,0:T(8,128)(2,1)S(1)} collective-permute-done((bf16[32,2048]{1,0:T(8,128)(2,1)S(1)}, bf16[32,2048]{1,0:T(8,128)(2,1)S(1)}, u32[]{:S(2)}, u32[]{:S(2)}) %collective-permute-start.11) | collective-permute-done | bytes 131104 | tf_op jit(solution)/shard_map/ppermute | solution.py:58
  47.4 2.2 %collective-permute-start.12 = (bf16[32,2048]{1,0:T(8,128)(2,1)}, bf16[32,2048]{1,0:T(8,128)(2,1)S(1)}, u32[]{:S(2)}, u32[]{:S(2)}) collective-permute-start(bf16[32,2048]{1,0:T(8,128)(2,1)} %get-tuple-element.43), channel_id=1, source_target_pairs={{0,28},{4,24},{8,20},{12,16},{16,12},{20,8},{24,4},{28,0},{1,29},{... | collective-permute-start | bytes 393224 | tf_op jit(solution)/shard_map/ppermute | solution.py:58
  50.5 6.2 %collective-permute-start.7 = (bf16[32,2048]{1,0:T(8,128)(2,1)}, bf16[32,2048]{1,0:T(8,128)(2,1)S(1)}, u32[]{:S(2)}, u32[]{:S(2)}) collective-permute-start(bf16[32,2048]{1,0:T(8,128)(2,1)} %get-tuple-element.38), channel_id=1, source_target_pairs={{0,8},{4,12},{8,0},{12,4},{16,24},{20,28},{24,16},{28,20},{1,9},{5... | collective-permute-start | bytes 393224 | tf_op jit(solution)/shard_map/ppermute | solution.py:58
  56.7 2.5 %collective-permute-start.9 = (bf16[32,2048]{1,0:T(8,128)(2,1)}, bf16[32,2048]{1,0:T(8,128)(2,1)S(1)}, u32[]{:S(2)}, u32[]{:S(2)}) collective-permute-start(bf16[32,2048]{1,0:T(8,128)(2,1)} %get-tuple-element.40), channel_id=1, source_target_pairs={{0,16},{4,20},{8,24},{12,28},{16,0},{20,4},{24,8},{28,12},{1,17},{... | collective-permute-start | bytes 393224 | tf_op jit(solution)/shard_map/ppermute | solution.py:58
  76.0 3.0 %shard_map.97 = (bf16[256,2048]{1,0:T(8,128)(2,1)S(1)}, bf16[256,512]{1,0:T(8,128)(2,1)S(1)}, bf16[256,256]{1,0:T(8,128)(2,1)S(1)}) custom-call(bf16[256,2048]{1,0:T(8,128)(2,1)} %bitcast.5.refs_0_.refs_6_, f32[512,512]{1,0:T(8,128)S(1)} %copy-done.1, bf16[2048,512]{1,0:T(8,128)(2,1)S(1)} %get-tuple-element.34.refs_2_.refs_9_, ...), custom_call_target="tpu_custom_call" | custom-call | flops 805306368 | bytes 6684672 | tf_op jit(solution)/shard_map/pallas_call | solution.py:26
  80.0 3.7 %shard_map.101 = (bf16[2,768,512]{2,1,0:T(8,128)(2,1)}, bf16[2,768,512]{2,1,0:T(8,128)(2,1)S(1)}) custom-call(bf16[512,2048]{1,0:T(8,128)(2,1)S(1)} %bitcast.17, bf16[256,512]{1,0:T(8,128)(2,1)S(1)} %copy-done.19, bf16[256,512]{1,0:T(8,128)(2,1)S(1)} %get-tuple-element.53.refs_2_, bf16[256,256]{1,0:T(8,128)(2,1)S(1)} %copy-done.33, ...), custom_call_target="tpu_custom_call" | custom-call | flops 1610612736 | bytes 8126464 | tf_op jit(solution)/shard_map/pallas_call | solution.py:26
  83.7 6.3 %all-to-all-start.1 = ((bf16[8,32,2048]{2,1,0:T(8,128)(2,1)}), bf16[8,32,2048]{2,1,0:T(8,128)(2,1)}, u32[]{:S(2)}, u32[]{:S(2)}) async-start(bf16[8,32,2048]{2,1,0:T(8,128)(2,1)} %bitcast.18), calls=%async_computation.1 | async-start | bytes 2097152 | tf_op jit(solution)/shard_map/all_to_all | solution.py:339
  96.2 2.4 %collective-permute-start.16 = (bf16[32,2048]{1,0:T(8,128)(2,1)S(1)}, bf16[32,2048]{1,0:T(8,128)(2,1)S(1)}, u32[]{:S(2)}, u32[]{:S(2)}) collective-permute-start(bf16[32,2048]{1,0:T(8,128)(2,1)S(1)} %copy-done.25), channel_id=1, source_target_pairs={{0,16},{4,20},{8,24},{12,28},{16,0},{20,4},{24,8},{28,12},{1,17},{... | collective-permute-start | bytes 393224 | tf_op jit(solution)/shard_map/ppermute | solution.py:58
  98.5 3.5 %collective-permute-done.13.refs_3_ = bf16[32,2048]{1,0:T(8,128)(2,1)S(1)} collective-permute-done((bf16[32,2048]{1,0:T(8,128)(2,1)S(1)}, bf16[32,2048]{1,0:T(8,128)(2,1)S(1)}, u32[]{:S(2)}, u32[]{:S(2)}) %collective-permute-start.13) | collective-permute-done | bytes 131104 | tf_op jit(solution)/shard_map/ppermute | solution.py:58
  102.1 4.0 %collective-permute-start.17 = (bf16[32,2048]{1,0:T(8,128)(2,1)S(1)}, bf16[32,2048]{1,0:T(8,128)(2,1)S(1)}, u32[]{:S(2)}, u32[]{:S(2)}) collective-permute-start(bf16[32,2048]{1,0:T(8,128)(2,1)S(1)} %copy-done.23), channel_id=1, source_target_pairs={{0,20},{4,16},{8,28},{12,24},{16,4},{20,0},{24,12},{28,8},{1,21},{... | collective-permute-start | bytes 393224 | tf_op jit(solution)/shard_map/ppermute | solution.py:58
  106.1 6.6 %collective-permute-done.14.refs_4_ = bf16[32,2048]{1,0:T(8,128)(2,1)S(1)} collective-permute-done((bf16[32,2048]{1,0:T(8,128)(2,1)S(1)}, bf16[32,2048]{1,0:T(8,128)(2,1)S(1)}, u32[]{:S(2)}, u32[]{:S(2)}) %collective-permute-start.14) | collective-permute-done | bytes 131104 | tf_op jit(solution)/shard_map/ppermute | solution.py:58
  112.8 1.8 %collective-permute-start.18 = (bf16[32,2048]{1,0:T(8,128)(2,1)S(1)}, bf16[32,2048]{1,0:T(8,128)(2,1)S(1)}, u32[]{:S(2)}, u32[]{:S(2)}) collective-permute-start(bf16[32,2048]{1,0:T(8,128)(2,1)S(1)} %copy-done.21), channel_id=1, source_target_pairs={{0,24},{4,28},{8,16},{12,20},{16,8},{20,12},{24,0},{28,4},{1,25},{... | collective-permute-start | bytes 393224 | tf_op jit(solution)/shard_map/ppermute | solution.py:58
  114.6 2.0 %collective-permute-done.15.refs_5_ = bf16[32,2048]{1,0:T(8,128)(2,1)S(1)} collective-permute-done((bf16[32,2048]{1,0:T(8,128)(2,1)S(1)}, bf16[32,2048]{1,0:T(8,128)(2,1)S(1)}, u32[]{:S(2)}, u32[]{:S(2)}) %collective-permute-start.15) | collective-permute-done | bytes 131104 | tf_op jit(solution)/shard_map/ppermute | solution.py:58
  118.3 10.0 %collective-permute-done.16.refs_6_ = bf16[32,2048]{1,0:T(8,128)(2,1)S(1)} collective-permute-done((bf16[32,2048]{1,0:T(8,128)(2,1)S(1)}, bf16[32,2048]{1,0:T(8,128)(2,1)S(1)}, u32[]{:S(2)}, u32[]{:S(2)}) %collective-permute-start.16) | collective-permute-done | bytes 131104 | tf_op jit(solution)/shard_map/ppermute | solution.py:58
  128.3 2.8 %collective-permute-done.17.refs_7_ = bf16[32,2048]{1,0:T(8,128)(2,1)S(1)} collective-permute-done((bf16[32,2048]{1,0:T(8,128)(2,1)S(1)}, bf16[32,2048]{1,0:T(8,128)(2,1)S(1)}, u32[]{:S(2)}, u32[]{:S(2)}) %collective-permute-start.17) | collective-permute-done | bytes 131104 | tf_op jit(solution)/shard_map/ppermute | solution.py:58
  131.1 4.4 %collective-permute-done.18.refs_8_ = bf16[32,2048]{1,0:T(8,128)(2,1)S(1)} collective-permute-done((bf16[32,2048]{1,0:T(8,128)(2,1)S(1)}, bf16[32,2048]{1,0:T(8,128)(2,1)S(1)}, u32[]{:S(2)}, u32[]{:S(2)}) %collective-permute-start.18) | collective-permute-done | bytes 131104 | tf_op jit(solution)/shard_map/ppermute | solution.py:58
  135.5 3.2 %collective-permute-done.19.refs_9_ = bf16[32,2048]{1,0:T(8,128)(2,1)S(1)} collective-permute-done((bf16[32,2048]{1,0:T(8,128)(2,1)S(1)}, bf16[32,2048]{1,0:T(8,128)(2,1)S(1)}, u32[]{:S(2)}, u32[]{:S(2)}) %collective-permute-start.19) | collective-permute-done | bytes 131104 | tf_op jit(solution)/shard_map/ppermute | solution.py:58
  139.8 2.3 %shard_map.100 = bf16[2,96,2048]{2,1,0:T(8,128)(2,1)} custom-call(s32[2,96]{1,0:T(2,128)S(1)} %bitcast.28, s32[2,96]{1,0:T(2,128)S(1)} %bitcast.32, bf16[256,2048]{1,0:T(8,128)(2,1)} %bitcast.10.refs_2_, bf16[2,96,2048]{2,1,0:T(8,128)(2,1)} %shard_map.99.refs_3_), custom_call_target="tpu_custom_call", output_to_operand_aliasing={{}: (3, {})} | custom-call | flops 100663296 | bytes 2622976 | tf_op jit(solution)/shard_map/pallas_call | solution.py:26
  142.1 2.2 %shard_map.103 = (bf16[512,512]{1,0:T(8,128)(2,1)}, bf16[64,2048]{1,0:T(8,128)(2,1)}) custom-call(bf16[2,768,512]{2,1,0:T(8,128)(2,1)S(1)} %get-tuple-element.57.ours_ref, bf16[2,768,512]{2,1,0:T(8,128)(2,1)S(1)} %collective-permute-done.20.near_ref, bf16[768,512]{1,0:T(8,128)(2,1)} %collective-permute-done.21.far_ref), custom_call_target="tpu_custom_call" | custom-call | bytes 4718592 | tf_op jit(solution)/shard_map/pallas_call | solution.py:26
  (102 shorter events, 37.5 us)
Async XLA Ops:
  7.9 66.8 %all-to-all-start = ((bf16[8,32,2048]{2,1,0:T(8,128)(2,1)}), bf16[8,32,2048]{2,1,0:T(8,128)(2,1)}, u32[]{:S(2)}, u32[]{:S(2)}) async-start(bf16[8,32,2048]{2,1,0:T(8,128)(2,1)} %bitcast.4), calls=%async_computation | async-start | bytes 2097152 | tf_op jit(solution)/shard_map/all_to_all | solution.py:339
  14.2 14.8 %collective-permute-start.1 = (bf16[512,512]{1,0:T(8,128)(2,1)S(1)}, bf16[512,512]{1,0:T(8,128)(2,1)S(1)}, u32[]{:S(2)}, u32[]{:S(2)}) collective-permute-start(bf16[512,512]{1,0:T(8,128)(2,1)S(1)} %bitcast.19), channel_id=1, source_target_pairs={{0,2},{1,3},{2,0},{3,1},{4,6},{5,7},{6,4},{7,5},{8,10},{9,11},{10,... | collective-permute-start | bytes 1572872 | tf_op jit(solution)/shard_map/ppermute | solution.py:58
  15.7 17.2 %collective-permute-start.4 = (bf16[64,2048]{1,0:T(8,128)(2,1)S(1)}, bf16[64,2048]{1,0:T(8,128)(2,1)S(1)}, u32[]{:S(2)}, u32[]{:S(2)}) collective-permute-start(bf16[64,2048]{1,0:T(8,128)(2,1)S(1)} %bitcast.22), channel_id=1, source_target_pairs={{0,2},{1,3},{2,0},{3,1},{4,6},{5,7},{6,4},{7,5},{8,10},{9,11},{10,... | collective-permute-start | bytes 786440 | tf_op jit(solution)/shard_map/ppermute | solution.py:58
  16.2 40.5 %collective-permute-start = (bf16[512,512]{1,0:T(8,128)(2,1)S(1)}, bf16[512,512]{1,0:T(8,128)(2,1)S(1)}, u32[]{:S(2)}, u32[]{:S(2)}) collective-permute-start(bf16[512,512]{1,0:T(8,128)(2,1)S(1)} %bitcast.20), channel_id=1, source_target_pairs={{0,1},{1,0},{2,3},{3,2},{4,5},{5,4},{6,7},{7,6},{8,9},{9,8},{10,11... | collective-permute-start | bytes 1572872 | tf_op jit(solution)/shard_map/ppermute | solution.py:58
  29.0 27.7 %collective-permute-start.2 = (bf16[512,512]{1,0:T(8,128)(2,1)S(1)}, bf16[512,512]{1,0:T(8,128)(2,1)S(1)}, u32[]{:S(2)}, u32[]{:S(2)}) collective-permute-start(bf16[512,512]{1,0:T(8,128)(2,1)S(1)} %collective-permute-done.1.refs_2_), channel_id=1, source_target_pairs={{0,1},{1,0},{2,3},{3,2},{4,5},{5,4},{6,7},{7,6},{8,9},{9,8},{10,11... | collective-permute-start | bytes 1572872 | tf_op jit(solution)/shard_map/ppermute | solution.py:58
  29.0 12.9 %collective-permute-start.10 = (bf16[32,2048]{1,0:T(8,128)(2,1)S(1)}, bf16[32,2048]{1,0:T(8,128)(2,1)S(1)}, u32[]{:S(2)}, u32[]{:S(2)}) collective-permute-start(bf16[32,2048]{1,0:T(8,128)(2,1)S(1)} %get-tuple-element.41), channel_id=1, source_target_pairs={{0,20},{4,16},{8,28},{12,24},{16,4},{20,0},{24,12},{28,8},{1,21},{... | collective-permute-start | bytes 393224 | tf_op jit(solution)/shard_map/ppermute | solution.py:58
  32.3 17.2 %collective-permute-start.3 = (bf16[64,2048]{1,0:T(8,128)(2,1)S(1)}, bf16[64,2048]{1,0:T(8,128)(2,1)S(1)}, u32[]{:S(2)}, u32[]{:S(2)}) collective-permute-start(bf16[64,2048]{1,0:T(8,128)(2,1)S(1)} %bitcast.23), channel_id=1, source_target_pairs={{0,1},{1,0},{2,3},{3,2},{4,5},{5,4},{6,7},{7,6},{8,9},{9,8},{10,11... | collective-permute-start | bytes 786440 | tf_op jit(solution)/shard_map/ppermute | solution.py:58
  32.9 17.5 %collective-permute-start.5 = (bf16[64,2048]{1,0:T(8,128)(2,1)S(1)}, bf16[64,2048]{1,0:T(8,128)(2,1)S(1)}, u32[]{:S(2)}, u32[]{:S(2)}) collective-permute-start(bf16[64,2048]{1,0:T(8,128)(2,1)S(1)} %collective-permute-done.4.refs_6_), channel_id=1, source_target_pairs={{0,1},{1,0},{2,3},{3,2},{4,5},{5,4},{6,7},{7,6},{8,9},{9,8},{10,11... | collective-permute-start | bytes 786440 | tf_op jit(solution)/shard_map/ppermute | solution.py:58
  41.9 5.4 %collective-permute-start.11 = (bf16[32,2048]{1,0:T(8,128)(2,1)S(1)}, bf16[32,2048]{1,0:T(8,128)(2,1)S(1)}, u32[]{:S(2)}, u32[]{:S(2)}) collective-permute-start(bf16[32,2048]{1,0:T(8,128)(2,1)S(1)} %get-tuple-element.42), channel_id=1, source_target_pairs={{0,24},{4,28},{8,16},{12,20},{16,8},{20,12},{24,0},{28,4},{1,25},{... | collective-permute-start | bytes 393224 | tf_op jit(solution)/shard_map/ppermute | solution.py:58
  47.4 15.9 %collective-permute-start.12 = (bf16[32,2048]{1,0:T(8,128)(2,1)}, bf16[32,2048]{1,0:T(8,128)(2,1)S(1)}, u32[]{:S(2)}, u32[]{:S(2)}) collective-permute-start(bf16[32,2048]{1,0:T(8,128)(2,1)} %get-tuple-element.43), channel_id=1, source_target_pairs={{0,28},{4,24},{8,20},{12,16},{16,12},{20,8},{24,4},{28,0},{1,29},{... | collective-permute-start | bytes 393224 | tf_op jit(solution)/shard_map/ppermute | solution.py:58
  49.5 13.8 %collective-permute-start.6 = (bf16[32,2048]{1,0:T(8,128)(2,1)}, bf16[32,2048]{1,0:T(8,128)(2,1)S(1)}, u32[]{:S(2)}, u32[]{:S(2)}) collective-permute-start(bf16[32,2048]{1,0:T(8,128)(2,1)} %get-tuple-element.37), channel_id=1, source_target_pairs={{0,4},{4,0},{8,12},{12,8},{16,20},{20,16},{24,28},{28,24},{1,5},{5... | collective-permute-start | bytes 393224 | tf_op jit(solution)/shard_map/ppermute | solution.py:58
  50.5 13.6 %collective-permute-start.7 = (bf16[32,2048]{1,0:T(8,128)(2,1)}, bf16[32,2048]{1,0:T(8,128)(2,1)S(1)}, u32[]{:S(2)}, u32[]{:S(2)}) collective-permute-start(bf16[32,2048]{1,0:T(8,128)(2,1)} %get-tuple-element.38), channel_id=1, source_target_pairs={{0,8},{4,12},{8,0},{12,4},{16,24},{20,28},{24,16},{28,20},{1,9},{5... | collective-permute-start | bytes 393224 | tf_op jit(solution)/shard_map/ppermute | solution.py:58
  56.7 9.1 %collective-permute-start.8 = (bf16[32,2048]{1,0:T(8,128)(2,1)}, bf16[32,2048]{1,0:T(8,128)(2,1)S(1)}, u32[]{:S(2)}, u32[]{:S(2)}) collective-permute-start(bf16[32,2048]{1,0:T(8,128)(2,1)} %get-tuple-element.39), channel_id=1, source_target_pairs={{0,12},{4,8},{8,4},{12,0},{16,28},{20,24},{24,20},{28,16},{1,13},{... | collective-permute-start | bytes 393224 | tf_op jit(solution)/shard_map/ppermute | solution.py:58
  56.7 9.1 %collective-permute-start.9 = (bf16[32,2048]{1,0:T(8,128)(2,1)}, bf16[32,2048]{1,0:T(8,128)(2,1)S(1)}, u32[]{:S(2)}, u32[]{:S(2)}) collective-permute-start(bf16[32,2048]{1,0:T(8,128)(2,1)} %get-tuple-element.40), channel_id=1, source_target_pairs={{0,16},{4,20},{8,24},{12,28},{16,0},{20,4},{24,8},{28,12},{1,17},{... | collective-permute-start | bytes 393224 | tf_op jit(solution)/shard_map/ppermute | solution.py:58
  83.7 6.3 %collective-permute-start.20 = (bf16[2,768,512]{2,1,0:T(8,128)(2,1)}, bf16[2,768,512]{2,1,0:T(8,128)(2,1)S(1)}, u32[]{:S(2)}, u32[]{:S(2)}) collective-permute-start(bf16[2,768,512]{2,1,0:T(8,128)(2,1)} %get-tuple-element.58), channel_id=1, source_target_pairs={{0,1},{1,0},{2,3},{3,2},{4,5},{5,4},{6,7},{7,6},{8,9},{9,8},{10,11... | collective-permute-start | bytes 4718600 | tf_op jit(solution)/shard_map/ppermute | solution.py:58
  83.7 56.1 %all-to-all-start.1 = ((bf16[8,32,2048]{2,1,0:T(8,128)(2,1)}), bf16[8,32,2048]{2,1,0:T(8,128)(2,1)}, u32[]{:S(2)}, u32[]{:S(2)}) async-start(bf16[8,32,2048]{2,1,0:T(8,128)(2,1)} %bitcast.18), calls=%async_computation.1 | async-start | bytes 2097152 | tf_op jit(solution)/shard_map/all_to_all | solution.py:339
  91.2 51.0 %collective-permute-start.21 = (bf16[768,512]{1,0:T(8,128)(2,1)}, bf16[768,512]{1,0:T(8,128)(2,1)}, u32[]{:S(2)}, u32[]{:S(2)}) collective-permute-start(bf16[768,512]{1,0:T(8,128)(2,1)} %shard_map.102), channel_id=1, source_target_pairs={{0,2},{1,3},{2,0},{3,1},{4,6},{5,7},{6,4},{7,5},{8,10},{9,11},{10,... | collective-permute-start | bytes 2359304 | tf_op jit(solution)/shard_map/ppermute | solution.py:58
  92.7 9.4 %collective-permute-start.13 = (bf16[32,2048]{1,0:T(8,128)(2,1)S(1)}, bf16[32,2048]{1,0:T(8,128)(2,1)S(1)}, u32[]{:S(2)}, u32[]{:S(2)}) collective-permute-start(bf16[32,2048]{1,0:T(8,128)(2,1)S(1)} %copy-done.31), channel_id=1, source_target_pairs={{0,4},{4,0},{8,12},{12,8},{16,20},{20,16},{24,28},{28,24},{1,5},{5... | collective-permute-start | bytes 393224 | tf_op jit(solution)/shard_map/ppermute | solution.py:58
  94.1 18.6 %collective-permute-start.14 = (bf16[32,2048]{1,0:T(8,128)(2,1)S(1)}, bf16[32,2048]{1,0:T(8,128)(2,1)S(1)}, u32[]{:S(2)}, u32[]{:S(2)}) collective-permute-start(bf16[32,2048]{1,0:T(8,128)(2,1)S(1)} %copy-done.29), channel_id=1, source_target_pairs={{0,8},{4,12},{8,0},{12,4},{16,24},{20,28},{24,16},{28,20},{1,9},{5... | collective-permute-start | bytes 393224 | tf_op jit(solution)/shard_map/ppermute | solution.py:58
  94.7 21.9 %collective-permute-start.15 = (bf16[32,2048]{1,0:T(8,128)(2,1)S(1)}, bf16[32,2048]{1,0:T(8,128)(2,1)S(1)}, u32[]{:S(2)}, u32[]{:S(2)}) collective-permute-start(bf16[32,2048]{1,0:T(8,128)(2,1)S(1)} %copy-done.27), channel_id=1, source_target_pairs={{0,12},{4,8},{8,4},{12,0},{16,28},{20,24},{24,20},{28,16},{1,13},{... | collective-permute-start | bytes 393224 | tf_op jit(solution)/shard_map/ppermute | solution.py:58
  96.2 32.1 %collective-permute-start.16 = (bf16[32,2048]{1,0:T(8,128)(2,1)S(1)}, bf16[32,2048]{1,0:T(8,128)(2,1)S(1)}, u32[]{:S(2)}, u32[]{:S(2)}) collective-permute-start(bf16[32,2048]{1,0:T(8,128)(2,1)S(1)} %copy-done.25), channel_id=1, source_target_pairs={{0,16},{4,20},{8,24},{12,28},{16,0},{20,4},{24,8},{28,12},{1,17},{... | collective-permute-start | bytes 393224 | tf_op jit(solution)/shard_map/ppermute | solution.py:58
  102.1 29.0 %collective-permute-start.17 = (bf16[32,2048]{1,0:T(8,128)(2,1)S(1)}, bf16[32,2048]{1,0:T(8,128)(2,1)S(1)}, u32[]{:S(2)}, u32[]{:S(2)}) collective-permute-start(bf16[32,2048]{1,0:T(8,128)(2,1)S(1)} %copy-done.23), channel_id=1, source_target_pairs={{0,20},{4,16},{8,28},{12,24},{16,4},{20,0},{24,12},{28,8},{1,21},{... | collective-permute-start | bytes 393224 | tf_op jit(solution)/shard_map/ppermute | solution.py:58
  112.8 22.7 %collective-permute-start.18 = (bf16[32,2048]{1,0:T(8,128)(2,1)S(1)}, bf16[32,2048]{1,0:T(8,128)(2,1)S(1)}, u32[]{:S(2)}, u32[]{:S(2)}) collective-permute-start(bf16[32,2048]{1,0:T(8,128)(2,1)S(1)} %copy-done.21), channel_id=1, source_target_pairs={{0,24},{4,28},{8,16},{12,20},{16,8},{20,12},{24,0},{28,4},{1,25},{... | collective-permute-start | bytes 393224 | tf_op jit(solution)/shard_map/ppermute | solution.py:58
  116.6 22.1 %collective-permute-start.19 = (bf16[32,2048]{1,0:T(8,128)(2,1)S(1)}, bf16[32,2048]{1,0:T(8,128)(2,1)S(1)}, u32[]{:S(2)}, u32[]{:S(2)}) collective-permute-start(bf16[32,2048]{1,0:T(8,128)(2,1)S(1)} %get-tuple-element.51), channel_id=1, source_target_pairs={{0,28},{4,24},{8,20},{12,16},{16,12},{20,8},{24,4},{28,0},{1,29},{... | collective-permute-start | bytes 393224 | tf_op jit(solution)/shard_map/ppermute | solution.py:58
  (34 other events, 199.1 us)

commit v2 on v1

--- a/solution.py
+++ b/solution.py
@@ -66,49 +66,63 @@
     return jnp.sum(jnp.where(down == across, spread, jnp.zeros_like(spread)), axis=1, keepdims=True)
 
 
-def relative_position(expert_ref, slot_ref, b, peer_slots, relative):
-    expert_row = expert_ref[b : b + 1, :]
+STEP = 512
+RELAYED = (0, 1)
+
+
+def row_tables(refs, b, peer_slots, relative):
+    if len(refs) == 3:
+        prob_ref, expert_ref, slot_ref = refs
+        prob = prob_ref[b : b + 1, :]
+        position = expert_ref[b : b + 1, :] * peer_slots + slot_ref[b : b + 1, :]
+    else:
+        (both_ref,) = refs
+        micro_count = both_ref.shape[0] // 2
+        prob = both_ref[b : b + 1, :]
+        position = both_ref[micro_count + b : micro_count + b + 1, :].astype(jnp.int32)
     if relative:
-        expert_row = expert_row ^ lax.axis_index("expert")
-    return expert_row * peer_slots + slot_ref[b : b + 1, :]
-
-
-STEP = 512
-
-
-def place_rows(out_grad, gate_prob, dest_expert, dest_slot, b, n_expert, peer_slots, relative, after):
-    rows, width = out_grad.shape[1:]
-    capacity = n_expert * peer_slots
-    operands = [out_grad, gate_prob, dest_expert, dest_slot]
-    in_specs = [pl.BlockSpec((1, rows, width), lambda i: (b, 0, 0))]
-    in_specs += [copied_spec(v.shape) for v in operands[1:]]
-    if after is not None:
-        operands.append(after)
-        in_specs.append(pl.BlockSpec(memory_space=pl.ANY))
-
-    def body(grad_ref, prob_ref, expert_ref, slot_ref, *refs):
-        out_refs = refs[-count:]
-        position = relative_position(expert_ref, slot_ref, b, peer_slots, relative)
-        slot_ids = lax.broadcasted_iota(jnp.int32, (capacity, rows), 0)
+        position = position ^ (lax.axis_index("expert") * peer_slots)
+    return prob, position
+
+
+def place_rows(grads, tables, b, peers, peer_slots, relative):
+    rows, width = grads.shape[1:]
+    slot_count = peers * peer_slots
+    count, block_rows = (peers, peer_slots) if relative else (1, slot_count)
+
+    def body(*refs):
+        out_refs, (grad_ref, *table_refs, sems) = refs[4 : 4 + count], refs[4 + count :]
+        copies = [pltpu.make_async_copy(refs[0].at[b], grad_ref, sems.at[0])]
+        copies += [
+            pltpu.make_async_copy(refs[1 + i], table_refs[i], sems.at[1 + i]) for i in range(3)
+        ]
+        for copy in copies:
+            copy.start()
+        for copy in copies[1:]:
+            copy.wait()
+        prob, position = row_tables(table_refs, b, peer_slots, relative)
+        slot_ids = lax.broadcasted_iota(jnp.int32, (slot_count, rows), 0)
         placing = jnp.where(slot_ids == position, 1.0, 0.0).astype(BF16)
-        prob = as_column(prob_ref[b : b + 1, :])
+        prob = as_column(prob)
+        copies[0].wait()
         for start in range(0, width, STEP):
             columns = slice(start, start + STEP)
-            weighted = (grad_ref[0, :, columns].astype(F32) * prob).astype(BF16)
+            weighted = (grad_ref[:, columns].astype(F32) * prob).astype(BF16)
             slots = jnp.dot(placing, weighted, preferred_element_type=F32).astype(BF16)
-            if relative:
-                for k in range(n_expert):
-                    out_refs[k][:, columns] = slots[k * peer_slots : (k + 1) * peer_slots]
-            else:
-                out_refs[0][:, columns] = slots
-
-    count, block_rows = (n_expert, peer_slots) if relative else (1, capacity)
-    return call(
-        body,
-        operands,
+            for k in range(count):
+                out_refs[k][:, columns] = slots[k * block_rows : (k + 1) * block_rows]
+
+    return call(
+        body,
+        [pltpu.with_memory_space_constraint(v, pltpu.HBM) for v in (grads, *tables)],
         [((block_rows, width), BF16)] * count,
-        flops=2 * capacity * rows * width,
-        in_specs=in_specs,
+        flops=2 * slot_count * rows * width,
+        in_specs=[pl.BlockSpec(memory_space=pltpu.HBM)] * 4,
+        scratch=[
+            pltpu.VMEM((rows, width), BF16),
+            *[pltpu.VMEM(v.shape, v.dtype) for v in tables],
+            pltpu.SemaphoreType.DMA((4,)),
+        ],
     )
 
 
@@ -197,46 +211,51 @@
     )
 
 
-def unplace_rows(back, dest_expert, dest_slot, b, n_expert, relative, rows, previous, micro_count):
-    width = back[0].shape[1]
-    count = len(back)
-    peer_slots = back[0].shape[0] if relative else back[0].shape[0] // n_expert
-    capacity = n_expert * peer_slots
+def collect_rows(blocks, tables, b, peers, peer_slots, relative, last=False, extras=(), previous=None):
+    width = blocks[0].shape[1]
+    micro_count, rows = tables[0].shape
+    count = len(blocks)
+    ahead = len(tables)
+    block_rows = blocks[0].shape[0]
+    slot_count = peers * peer_slots
 
     def body(*refs):
-        expert_ref, slot_ref = refs[:2]
-        blocks = refs[2 : 2 + count]
-        out_ref = refs[-2] if relative else refs[-1]
-        position = as_column(relative_position(expert_ref, slot_ref, b, peer_slots, relative))
-        slot_ids = lax.broadcasted_iota(jnp.int32, (rows, capacity), 1)
+        block_refs = refs[ahead : ahead + count]
+        extra_refs = refs[ahead + count : ahead + count + len(extras)]
+        out_ref, stage = refs[-2:]
+        position = as_column(row_tables(refs[:ahead], b, peer_slots, relative)[1])
+        slot_ids = lax.broadcasted_iota(jnp.int32, (rows, slot_count), 1)
         taking = jnp.where(slot_ids == position, 1.0, 0.0).astype(BF16)
-        if relative:
-            stage = refs[-1]
-            for k in range(n_expert):
-                stage[k * peer_slots : (k + 1) * peer_slots, :] = blocks[k][...]
-        else:
-            stage = blocks[0]
+        for k in range(count):
+            stage[k * block_rows : (k + 1) * block_rows, :] = block_refs[k][...]
         for start in range(0, width, STEP):
             columns = slice(start, start + STEP)
-            out_ref[0, :, columns] = jnp.dot(
-                taking, stage[:, columns], preferred_element_type=F32
-            ).astype(BF16)
-
-    operands = [dest_expert, dest_slot, *back]
-    in_specs = [copied_spec(v.shape) for v in operands[:2]] + [resident_spec()] * count
-    aliases = {}
-    if previous is not None:
-        aliases = {len(operands): 0}
-        operands.append(previous)
-        in_specs.append(pl.BlockSpec(memory_space=pl.ANY))
+            taken = jnp.dot(taking, stage[:, columns], preferred_element_type=F32)
+            for ref in extra_refs:
+                taken = taken + ref[:, columns].astype(F32)
+            if last:
+                out_ref[0, :, columns] = taken.astype(BF16)
+            else:
+                out_ref[:, columns] = taken.astype(BF16)
+
+    operands = [*tables, *blocks, *extras]
+    in_specs = [resident_spec()] * len(operands)
+    out_shape, out_specs, aliases = (rows, width), None, {}
+    if last:
+        out_shape = (micro_count, rows, width)
+        out_specs = [pl.BlockSpec((1, rows, width), lambda i: (b, 0, 0))]
+        if previous is not None:
+            aliases = {len(operands): 0}
+            operands.append(previous)
+            in_specs.append(pl.BlockSpec(memory_space=pl.ANY))
     return call(
         body,
         operands,
-        [((micro_count, rows, width), BF16)],
-        flops=2 * capacity * rows * width,
+        [(out_shape, BF16)],
+        flops=2 * slot_count * rows * width,
         in_specs=in_specs,
-        out_specs=[pl.BlockSpec((1, rows, width), lambda i: (b, 0, 0))],
-        scratch=[pltpu.VMEM((capacity, width), BF16)] if relative else [],
+        out_specs=out_specs,
+        scratch=[pltpu.VMEM((slot_count, width), BF16)],
         aliases=aliases,
     )[0]
 
@@ -323,52 +342,65 @@
     capacity = x_saved.shape[3]
     width = x_saved.shape[4]
     peer_slots = capacity // n_expert
-    rows = out_grad.shape[3]
-    small = n_expert <= 16
-    permuted = [small and b % 2 == 0 for b in range(micro_count)]
-    order = sorted(range(1, n_expert), key=lambda k: -k)
-
-    def exchange(blocks, relative):
-        if relative:
-            moved = {0: blocks[0]}
-            for k in order:
-                moved[k] = swap(blocks[k], "expert", k)
-            return [moved[k] for k in range(n_expert)]
-        value = blocks[0]
+    relay = n_expert in (4, 8, 16)
+    half = n_expert // 2
+    micros = range(micro_count)
+
+    def send(value, bit):
+        return swap(value, "expert", bit)
+
+    def exchange(value):
         parts = value.reshape(n_expert, peer_slots, width)
         moved = lax.all_to_all(parts, "expert", split_axis=0, concat_axis=0, tiled=True)
-        return [moved.reshape(value.shape)]
-
-    grad, prob = out_grad[0, 0], gate_prob[0, 0]
-    expert, slot = dest_expert[0, 0], dest_slot[0, 0]
+        return moved.reshape(value.shape)
+
+    grads = out_grad[0, 0]
+    tables = [gate_prob[0, 0], dest_expert[0, 0], dest_slot[0, 0]]
     saved = x_saved[0, 0].reshape(micro_count * capacity, width)
     pieces_gu, pieces_down = gather_pieces([w_gate_up[0], w_down[0]])
     arrived = []
-    after = None
-    for b in range(micro_count):
-        placed = place_rows(grad, prob, expert, slot, b, n_expert, peer_slots, permuted[b], after)
-        after = placed[0]
-        arrived.append(exchange(placed, permuted[b]))
+    order = [half, *range(half - 1, 0, -1), *range(half + 1, n_expert)]
+    for b in micros:
+        blocks = place_rows(grads, tables, b, n_expert, peer_slots, relay)
+        if relay:
+            turns = order if b == 0 else [*range(half, n_expert), *range(half - 1, 0, -1)]
+            moved = {k: send(blocks[k], k) for k in turns}
+            arrived.append([blocks[0]] + [moved[k] for k in range(1, n_expert)])
+        else:
+            arrived.append([exchange(blocks[0])])
+    if relay:
+        position = tables[1] * peer_slots + tables[2]
+        far_tables = [send(jnp.concatenate([tables[0], position.astype(F32)]), half)]
     full_gu, full_down, gate_up = prepare(pieces_gu, pieces_down, saved)
 
     hidden_all, gu_all, slot_all, backs = [], [], [], []
-    for b in range(micro_count):
-        results = expert_rows(arrived[b], gate_up, full_gu, full_down, b, n_expert, permuted[b])
+    for b in micros:
+        results = expert_rows(arrived[b], gate_up, full_gu, full_down, b, n_expert, relay)
         count = len(arrived[b])
         gu_all.append(results[count])
         hidden_all.append(results[count + 1])
-        slot_all.append(results[count + 2] if permuted[b] else arrived[b][0])
-        backs.append(exchange(results[:count], permuted[b]))
+        slot_all.append(results[count + 2] if relay else arrived[b][0])
+        backs.append(results[:count])
+    in_rows = None
+    for b in micros:
+        blocks, extras, peers = backs[b], [], n_expert
+        if not relay:
+            near = [exchange(blocks[0])]
+        elif b not in RELAYED:
+            moved = {k: send(blocks[k], k) for k in order}
+            near = [blocks[0]] + [moved[k] for k in range(1, n_expert)]
+        else:
+            handed = [blocks[half]] + [send(blocks[half + k], k) for k in range(1, half)]
+            near = [blocks[0]] + [send(blocks[k], k) for k in range(1, half)]
+            others = collect_rows(handed, far_tables, b, half, peer_slots, True)
+            extras = [send(others, half)]
+            peers = half
+        in_rows = collect_rows(near, tables, b, peers, peer_slots, relay, True, extras, in_rows)
     near, ours = weight_parts(saved, gu_all, hidden_all, slot_all)
     got_near = swap(near, "mirror", 1)
     pair = near_sum(ours, got_near)
     got_far = swap(pair, "mirror", 2)
     share_gu, share_down = final_sum(ours, got_near, got_far, w_gate_up.shape[1], w_down.shape[1])
-    in_rows = None
-    for b in range(micro_count):
-        in_rows = unplace_rows(
-            backs[b], expert, slot, b, n_expert, permuted[b], rows, in_rows, micro_count
-        )
     return (in_rows[None, None], share_gu[None], share_down[None])
 
 

time: 145 us -> 128 us (0.88)
  the two profiles are of different devices: /device:TPU:8 before, /device:TPU:0 now
where the time goes in v2:
time: 128 us
  starting transfers between devices  62.9 us (49%)
  waiting for transfers between devices  48.9 us (38%)
  Pallas kernels  13.7 us (11%)
  local copies, waits for them, and re-layouts  1.62 us (1%)
    ppermute x37, starting transfers between devices, swap(): return lax.ppermute(value, axis, [(i, i ^ bit) for i in range(size)])  62.9 us
    ppermute x37, waiting for transfers between devices, swap(): return lax.ppermute(value, axis, [(i, i ^ bit) for i in range(size)])  48.9 us
    pallas_call x12, Pallas kernels, call(): pl.pallas_call(body, grid=(steps,), in_specs=in_specs or [resident_spec()...  13.7 us
  transfers between devices with their start and end apart: 37, of which 15 were waited for; matrix products, arithmetic and copies ran while one was open for 0% of the time, Pallas kernels for 7%

profile of v2, /device:TPU:0, one launch (start us, length us, event | category | flops | bytes accessed | tf_op | source)
XLA Modules:
  0.0 127.9 jit_solution(7035272972836409709)
XLA Ops:
  0.7 3.0 %collective-permute-start.8 = (bf16[512,512]{1,0:T(8,128)(2,1)}, bf16[512,512]{1,0:T(8,128)(2,1)S(1)}, u32[]{:S(2)}, u32[]{:S(2)}) collective-permute-start(bf16[512,512]{1,0:T(8,128)(2,1)} %bitcast.14), channel_id=1, source_target_pairs={{0,2},{1,3},{2,0},{3,1},{4,6},{5,7},{6,4},{7,5},{8,10},{9,11},{10,... | collective-permute-start | bytes 1572872 | tf_op jit(solution)/shard_map/ppermute | solution.py:58
  8.7 2.6 %collective-permute-start.3 = (bf16[32,2048]{1,0:T(8,128)(2,1)S(1)}, bf16[32,2048]{1,0:T(8,128)(2,1)S(1)}, u32[]{:S(2)}, u32[]{:S(2)}) collective-permute-start(bf16[32,2048]{1,0:T(8,128)(2,1)S(1)} %get-tuple-element.52), channel_id=1, source_target_pairs={{0,16},{4,20},{8,24},{12,28},{16,0},{20,4},{24,8},{28,12},{1,17},{... | collective-permute-start | bytes 393224 | tf_op jit(solution)/shard_map/ppermute | solution.py:58
  11.3 3.0 %collective-permute-start.4 = (bf16[32,2048]{1,0:T(8,128)(2,1)S(1)}, bf16[32,2048]{1,0:T(8,128)(2,1)S(1)}, u32[]{:S(2)}, u32[]{:S(2)}) collective-permute-start(bf16[32,2048]{1,0:T(8,128)(2,1)S(1)} %get-tuple-element.53), channel_id=1, source_target_pairs={{0,20},{4,16},{8,28},{12,24},{16,4},{20,0},{24,12},{28,8},{1,21},{... | collective-permute-start | bytes 393224 | tf_op jit(solution)/shard_map/ppermute | solution.py:58
  14.2 2.3 %collective-permute-done.1.refs_2_ = bf16[32,2048]{1,0:T(8,128)(2,1)S(1)} collective-permute-done((bf16[32,2048]{1,0:T(8,128)(2,1)S(1)}, bf16[32,2048]{1,0:T(8,128)(2,1)S(1)}, u32[]{:S(2)}, u32[]{:S(2)}) %collective-permute-start.1) | collective-permute-done | bytes 131104 | tf_op jit(solution)/shard_map/ppermute | solution.py:58
  18.4 6.3 %collective-permute-start.5 = (bf16[32,2048]{1,0:T(8,128)(2,1)S(1)}, bf16[32,2048]{1,0:T(8,128)(2,1)S(1)}, u32[]{:S(2)}, u32[]{:S(2)}) collective-permute-start(bf16[32,2048]{1,0:T(8,128)(2,1)S(1)} %get-tuple-element.54), channel_id=1, source_target_pairs={{0,24},{4,28},{8,16},{12,20},{16,8},{20,12},{24,0},{28,4},{1,25},{... | collective-permute-start | bytes 393224 | tf_op jit(solution)/shard_map/ppermute | solution.py:58
  25.4 4.4 %collective-permute-start.6 = (bf16[32,2048]{1,0:T(8,128)(2,1)S(1)}, bf16[32,2048]{1,0:T(8,128)(2,1)S(1)}, u32[]{:S(2)}, u32[]{:S(2)}) collective-permute-start(bf16[32,2048]{1,0:T(8,128)(2,1)S(1)} %get-tuple-element.55), channel_id=1, source_target_pairs={{0,28},{4,24},{8,20},{12,16},{16,12},{20,8},{24,4},{28,0},{1,29},{... | collective-permute-start | bytes 393224 | tf_op jit(solution)/shard_map/ppermute | solution.py:58
  33.7 2.6 %collective-permute-done.21.refs_1_ = bf16[32,2048]{1,0:T(8,128)(2,1)S(1)} collective-permute-done((bf16[32,2048]{1,0:T(8,128)(2,1)S(1)}, bf16[32,2048]{1,0:T(8,128)(2,1)S(1)}, u32[]{:S(2)}, u32[]{:S(2)}) %collective-permute-start.21) | collective-permute-done | bytes 131104 | tf_op jit(solution)/shard_map/ppermute | solution.py:58
  37.9 3.5 %collective-permute-done.22.refs_2_ = bf16[32,2048]{1,0:T(8,128)(2,1)S(1)} collective-permute-done((bf16[32,2048]{1,0:T(8,128)(2,1)S(1)}, bf16[32,2048]{1,0:T(8,128)(2,1)S(1)}, u32[]{:S(2)}, u32[]{:S(2)}) %collective-permute-start.22) | collective-permute-done | bytes 131104 | tf_op jit(solution)/shard_map/ppermute | solution.py:58
  41.4 3.6 %collective-permute-start.23 = (bf16[32,2048]{1,0:T(8,128)(2,1)S(1)}, bf16[32,2048]{1,0:T(8,128)(2,1)S(1)}, u32[]{:S(2)}, u32[]{:S(2)}) collective-permute-start(bf16[32,2048]{1,0:T(8,128)(2,1)S(1)} %get-tuple-element.70), channel_id=1, source_target_pairs={{0,12},{4,8},{8,4},{12,0},{16,28},{20,24},{24,20},{28,16},{1,13},{... | collective-permute-start | bytes 393224 | tf_op jit(solution)/shard_map/ppermute | solution.py:58
  46.8 2.0 %collective-permute-start.26 = (bf16[32,2048]{1,0:T(8,128)(2,1)S(1)}, bf16[32,2048]{1,0:T(8,128)(2,1)S(1)}, u32[]{:S(2)}, u32[]{:S(2)}) collective-permute-start(bf16[32,2048]{1,0:T(8,128)(2,1)S(1)} %get-tuple-element.73), channel_id=1, source_target_pairs={{0,24},{4,28},{8,16},{12,20},{16,8},{20,12},{24,0},{28,4},{1,25},{... | collective-permute-start | bytes 393224 | tf_op jit(solution)/shard_map/ppermute | solution.py:58
  48.8 3.8 %collective-permute-start.27 = (bf16[32,2048]{1,0:T(8,128)(2,1)S(1)}, bf16[32,2048]{1,0:T(8,128)(2,1)S(1)}, u32[]{:S(2)}, u32[]{:S(2)}) collective-permute-start(bf16[32,2048]{1,0:T(8,128)(2,1)S(1)} %get-tuple-element.74), channel_id=1, source_target_pairs={{0,28},{4,24},{8,20},{12,16},{16,12},{20,8},{24,4},{28,0},{1,29},{... | collective-permute-start | bytes 393224 | tf_op jit(solution)/shard_map/ppermute | solution.py:58
  57.3 3.2 %collective-permute-done.24.refs_4_ = bf16[32,2048]{1,0:T(8,128)(2,1)S(1)} collective-permute-done((bf16[32,2048]{1,0:T(8,128)(2,1)S(1)}, bf16[32,2048]{1,0:T(8,128)(2,1)S(1)}, u32[]{:S(2)}, u32[]{:S(2)}) %collective-permute-start.24) | collective-permute-done | bytes 131104 | tf_op jit(solution)/shard_map/ppermute | solution.py:58
  60.6 2.5 %collective-permute-done.25.refs_5_ = bf16[32,2048]{1,0:T(8,128)(2,1)S(1)} collective-permute-done((bf16[32,2048]{1,0:T(8,128)(2,1)S(1)}, bf16[32,2048]{1,0:T(8,128)(2,1)S(1)}, u32[]{:S(2)}, u32[]{:S(2)}) %collective-permute-start.25) | collective-permute-done | bytes 131104 | tf_op jit(solution)/shard_map/ppermute | solution.py:58
  64.8 1.9 %shard_map.103 = (bf16[2,768,512]{2,1,0:T(8,128)(2,1)S(1)}, bf16[2,768,512]{2,1,0:T(8,128)(2,1)S(1)}) custom-call(bf16[512,2048]{1,0:T(8,128)(2,1)S(1)} %bitcast.13, bf16[256,512]{1,0:T(8,128)(2,1)S(1)} %get-tuple-element.83.refs_1_, bf16[256,512]{1,0:T(8,128)(2,1)S(1)} %get-tuple-element.84.refs_2_, bf16[256,256]{1,0:T(8,128)(2,1)S(1)} %get-tuple-element.85.refs_3_, ...), custom_call_target="tpu_custom_call" | custom-call | flops 1610612736 | bytes 8126464 | tf_op jit(solution)/shard_map/pallas_call | solution.py:26
  68.6 3.5 %collective-permute-start.32 = (bf16[32,2048]{1,0:T(8,128)(2,1)S(1)}, bf16[32,2048]{1,0:T(8,128)(2,1)S(1)}, u32[]{:S(2)}, u32[]{:S(2)}) collective-permute-start(bf16[32,2048]{1,0:T(8,128)(2,1)S(1)} %get-tuple-element.81), channel_id=1, source_target_pairs={{0,8},{4,12},{8,0},{12,4},{16,24},{20,28},{24,16},{28,20},{1,9},{5... | collective-permute-start | bytes 393224 | tf_op jit(solution)/shard_map/ppermute | solution.py:58
  73.7 3.1 %collective-permute-start.16 = (f32[4,96]{1,0:T(4,128)S(1)}, f32[4,96]{1,0:T(4,128)S(1)}, u32[]{:S(2)}, u32[]{:S(2)}) collective-permute-start(f32[4,96]{1,0:T(4,128)S(1)} %pad_maximum_fusion), channel_id=1, source_target_pairs={{0,16},{4,20},{8,24},{12,28},{16,0},{20,4},{24,8},{28,12},{1,17},{... | collective-permute-start | bytes 4616 | tf_op jit(solution)/shard_map/ppermute | solution.py:58
  79.3 3.4 %collective-permute-start.18 = (bf16[32,2048]{1,0:T(8,128)(2,1)S(1)}, bf16[32,2048]{1,0:T(8,128)(2,1)S(1)}, u32[]{:S(2)}, u32[]{:S(2)}) collective-permute-start(bf16[32,2048]{1,0:T(8,128)(2,1)S(1)} %get-tuple-element.65), channel_id=1, source_target_pairs={{0,8},{4,12},{8,0},{12,4},{16,24},{20,28},{24,16},{28,20},{1,9},{5... | collective-permute-start | bytes 393224 | tf_op jit(solution)/shard_map/ppermute | solution.py:58
  86.4 3.0 %collective-permute-done.18.refs_3_ = bf16[32,2048]{1,0:T(8,128)(2,1)S(1)} collective-permute-done((bf16[32,2048]{1,0:T(8,128)(2,1)S(1)}, bf16[32,2048]{1,0:T(8,128)(2,1)S(1)}, u32[]{:S(2)}, u32[]{:S(2)}) %collective-permute-start.18) | collective-permute-done | bytes 131104 | tf_op jit(solution)/shard_map/ppermute | solution.py:58
  89.4 2.7 %collective-permute-done.19.refs_4_ = bf16[32,2048]{1,0:T(8,128)(2,1)S(1)} collective-permute-done((bf16[32,2048]{1,0:T(8,128)(2,1)S(1)}, bf16[32,2048]{1,0:T(8,128)(2,1)S(1)}, u32[]{:S(2)}, u32[]{:S(2)}) %collective-permute-start.19) | collective-permute-done | bytes 131104 | tf_op jit(solution)/shard_map/ppermute | solution.py:58
  92.8 2.7 %collective-permute-start.29 = (bf16[32,2048]{1,0:T(8,128)(2,1)S(1)}, bf16[32,2048]{1,0:T(8,128)(2,1)S(1)}, u32[]{:S(2)}, u32[]{:S(2)}) collective-permute-start(bf16[32,2048]{1,0:T(8,128)(2,1)S(1)} %get-tuple-element.77), channel_id=1, source_target_pairs={{0,8},{4,12},{8,0},{12,4},{16,24},{20,28},{24,16},{28,20},{1,9},{5... | collective-permute-start | bytes 393224 | tf_op jit(solution)/shard_map/ppermute | solution.py:58
  96.2 12.4 %collective-permute-done.29.refs_5_ = bf16[32,2048]{1,0:T(8,128)(2,1)S(1)} collective-permute-done((bf16[32,2048]{1,0:T(8,128)(2,1)S(1)}, bf16[32,2048]{1,0:T(8,128)(2,1)S(1)}, u32[]{:S(2)}, u32[]{:S(2)}) %collective-permute-start.29) | collective-permute-done | bytes 131104 | tf_op jit(solution)/shard_map/ppermute | solution.py:58
  110.1 2.9 %collective-permute-start.14 = (bf16[32,2048]{1,0:T(8,128)(2,1)S(1)}, bf16[32,2048]{1,0:T(8,128)(2,1)S(1)}, u32[]{:S(2)}, u32[]{:S(2)}) collective-permute-start(bf16[32,2048]{1,0:T(8,128)(2,1)S(1)} %get-tuple-element.61), channel_id=1, source_target_pairs={{0,8},{4,12},{8,0},{12,4},{16,24},{20,28},{24,16},{28,20},{1,9},{5... | collective-permute-start | bytes 393224 | tf_op jit(solution)/shard_map/ppermute | solution.py:58
  114.6 7.9 %collective-permute-done.14.refs_5_ = bf16[32,2048]{1,0:T(8,128)(2,1)S(1)} collective-permute-done((bf16[32,2048]{1,0:T(8,128)(2,1)S(1)}, bf16[32,2048]{1,0:T(8,128)(2,1)S(1)}, u32[]{:S(2)}, u32[]{:S(2)}) %collective-permute-start.14) | collective-permute-done | bytes 131104 | tf_op jit(solution)/shard_map/ppermute | solution.py:58
  122.5 3.2 %collective-permute-done.15.refs_6_ = bf16[32,2048]{1,0:T(8,128)(2,1)S(1)} collective-permute-done((bf16[32,2048]{1,0:T(8,128)(2,1)S(1)}, bf16[32,2048]{1,0:T(8,128)(2,1)S(1)}, u32[]{:S(2)}, u32[]{:S(2)}) %collective-permute-start.15) | collective-permute-done | bytes 131104 | tf_op jit(solution)/shard_map/ppermute | solution.py:58
  (78 shorter events, 37.6 us)
Async XLA Ops:
  0.7 17.7 %collective-permute-start.8 = (bf16[512,512]{1,0:T(8,128)(2,1)}, bf16[512,512]{1,0:T(8,128)(2,1)S(1)}, u32[]{:S(2)}, u32[]{:S(2)}) collective-permute-start(bf16[512,512]{1,0:T(8,128)(2,1)} %bitcast.14), channel_id=1, source_target_pairs={{0,2},{1,3},{2,0},{3,1},{4,6},{5,7},{6,4},{7,5},{8,10},{9,11},{10,... | collective-permute-start | bytes 1572872 | tf_op jit(solution)/shard_map/ppermute | solution.py:58
  11.3 14.1 %collective-permute-start.4 = (bf16[32,2048]{1,0:T(8,128)(2,1)S(1)}, bf16[32,2048]{1,0:T(8,128)(2,1)S(1)}, u32[]{:S(2)}, u32[]{:S(2)}) collective-permute-start(bf16[32,2048]{1,0:T(8,128)(2,1)S(1)} %get-tuple-element.53), channel_id=1, source_target_pairs={{0,20},{4,16},{8,28},{12,24},{16,4},{20,0},{24,12},{28,8},{1,21},{... | collective-permute-start | bytes 393224 | tf_op jit(solution)/shard_map/ppermute | solution.py:58
  16.6 28.4 %collective-permute-start.7 = (bf16[512,512]{1,0:T(8,128)(2,1)}, bf16[512,512]{1,0:T(8,128)(2,1)S(1)}, u32[]{:S(2)}, u32[]{:S(2)}) collective-permute-start(bf16[512,512]{1,0:T(8,128)(2,1)} %bitcast.15), channel_id=1, source_target_pairs={{0,1},{1,0},{2,3},{3,2},{4,5},{5,4},{6,7},{7,6},{8,9},{9,8},{10,11... | collective-permute-start | bytes 1572872 | tf_op jit(solution)/shard_map/ppermute | solution.py:58
  18.3 14.9 %collective-permute-start.11 = (bf16[64,2048]{1,0:T(8,128)(2,1)}, bf16[64,2048]{1,0:T(8,128)(2,1)S(1)}, u32[]{:S(2)}, u32[]{:S(2)}) collective-permute-start(bf16[64,2048]{1,0:T(8,128)(2,1)} %bitcast.17), channel_id=1, source_target_pairs={{0,2},{1,3},{2,0},{3,1},{4,6},{5,7},{6,4},{7,5},{8,10},{9,11},{10,... | collective-permute-start | bytes 786440 | tf_op jit(solution)/shard_map/ppermute | solution.py:58
  18.4 30.5 %collective-permute-start.9 = (bf16[512,512]{1,0:T(8,128)(2,1)S(1)}, bf16[512,512]{1,0:T(8,128)(2,1)S(1)}, u32[]{:S(2)}, u32[]{:S(2)}) collective-permute-start(bf16[512,512]{1,0:T(8,128)(2,1)S(1)} %collective-permute-done.8.refs_2_), channel_id=1, source_target_pairs={{0,1},{1,0},{2,3},{3,2},{4,5},{5,4},{6,7},{7,6},{8,9},{9,8},{10,11... | collective-permute-start | bytes 1572872 | tf_op jit(solution)/shard_map/ppermute | solution.py:58
  18.4 12.9 %collective-permute-start.5 = (bf16[32,2048]{1,0:T(8,128)(2,1)S(1)}, bf16[32,2048]{1,0:T(8,128)(2,1)S(1)}, u32[]{:S(2)}, u32[]{:S(2)}) collective-permute-start(bf16[32,2048]{1,0:T(8,128)(2,1)S(1)} %get-tuple-element.54), channel_id=1, source_target_pairs={{0,24},{4,28},{8,16},{12,20},{16,8},{20,12},{24,0},{28,4},{1,25},{... | collective-permute-start | bytes 393224 | tf_op jit(solution)/shard_map/ppermute | solution.py:58
  33.2 11.8 %collective-permute-start.10 = (bf16[64,2048]{1,0:T(8,128)(2,1)S(1)}, bf16[64,2048]{1,0:T(8,128)(2,1)S(1)}, u32[]{:S(2)}, u32[]{:S(2)}) collective-permute-start(bf16[64,2048]{1,0:T(8,128)(2,1)S(1)} %bitcast.18), channel_id=1, source_target_pairs={{0,1},{1,0},{2,3},{3,2},{4,5},{5,4},{6,7},{7,6},{8,9},{9,8},{10,11... | collective-permute-start | bytes 786440 | tf_op jit(solution)/shard_map/ppermute | solution.py:58
  33.2 13.6 %collective-permute-start.12 = (bf16[64,2048]{1,0:T(8,128)(2,1)S(1)}, bf16[64,2048]{1,0:T(8,128)(2,1)S(1)}, u32[]{:S(2)}, u32[]{:S(2)}) collective-permute-start(bf16[64,2048]{1,0:T(8,128)(2,1)S(1)} %collective-permute-done.11.refs_6_), channel_id=1, source_target_pairs={{0,1},{1,0},{2,3},{3,2},{4,5},{5,4},{6,7},{7,6},{8,9},{9,8},{10,11... | collective-permute-start | bytes 786440 | tf_op jit(solution)/shard_map/ppermute | solution.py:58
  41.4 15.9 %collective-permute-start.23 = (bf16[32,2048]{1,0:T(8,128)(2,1)S(1)}, bf16[32,2048]{1,0:T(8,128)(2,1)S(1)}, u32[]{:S(2)}, u32[]{:S(2)}) collective-permute-start(bf16[32,2048]{1,0:T(8,128)(2,1)S(1)} %get-tuple-element.70), channel_id=1, source_target_pairs={{0,12},{4,8},{8,4},{12,0},{16,28},{20,24},{24,20},{28,16},{1,13},{... | collective-permute-start | bytes 393224 | tf_op jit(solution)/shard_map/ppermute | solution.py:58
  44.9 15.6 %collective-permute-start.24 = (bf16[32,2048]{1,0:T(8,128)(2,1)S(1)}, bf16[32,2048]{1,0:T(8,128)(2,1)S(1)}, u32[]{:S(2)}, u32[]{:S(2)}) collective-permute-start(bf16[32,2048]{1,0:T(8,128)(2,1)S(1)} %get-tuple-element.71), channel_id=1, source_target_pairs={{0,16},{4,20},{8,24},{12,28},{16,0},{20,4},{24,8},{28,12},{1,17},{... | collective-permute-start | bytes 393224 | tf_op jit(solution)/shard_map/ppermute | solution.py:58
  45.0 18.1 %collective-permute-start.25 = (bf16[32,2048]{1,0:T(8,128)(2,1)S(1)}, bf16[32,2048]{1,0:T(8,128)(2,1)S(1)}, u32[]{:S(2)}, u32[]{:S(2)}) collective-permute-start(bf16[32,2048]{1,0:T(8,128)(2,1)S(1)} %get-tuple-element.72), channel_id=1, source_target_pairs={{0,20},{4,16},{8,28},{12,24},{16,4},{20,0},{24,12},{28,8},{1,21},{... | collective-permute-start | bytes 393224 | tf_op jit(solution)/shard_map/ppermute | solution.py:58
  46.8 16.3 %collective-permute-start.26 = (bf16[32,2048]{1,0:T(8,128)(2,1)S(1)}, bf16[32,2048]{1,0:T(8,128)(2,1)S(1)}, u32[]{:S(2)}, u32[]{:S(2)}) collective-permute-start(bf16[32,2048]{1,0:T(8,128)(2,1)S(1)} %get-tuple-element.73), channel_id=1, source_target_pairs={{0,24},{4,28},{8,16},{12,20},{16,8},{20,12},{24,0},{28,4},{1,25},{... | collective-permute-start | bytes 393224 | tf_op jit(solution)/shard_map/ppermute | solution.py:58
  48.8 14.2 %collective-permute-start.27 = (bf16[32,2048]{1,0:T(8,128)(2,1)S(1)}, bf16[32,2048]{1,0:T(8,128)(2,1)S(1)}, u32[]{:S(2)}, u32[]{:S(2)}) collective-permute-start(bf16[32,2048]{1,0:T(8,128)(2,1)S(1)} %get-tuple-element.74), channel_id=1, source_target_pairs={{0,28},{4,24},{8,20},{12,16},{16,12},{20,8},{24,4},{28,0},{1,29},{... | collective-permute-start | bytes 393224 | tf_op jit(solution)/shard_map/ppermute | solution.py:58
  66.8 12.6 %collective-permute-start.31 = (bf16[32,2048]{1,0:T(8,128)(2,1)S(1)}, bf16[32,2048]{1,0:T(8,128)(2,1)S(1)}, u32[]{:S(2)}, u32[]{:S(2)}) collective-permute-start(bf16[32,2048]{1,0:T(8,128)(2,1)S(1)} %get-tuple-element.80), channel_id=1, source_target_pairs={{0,4},{4,0},{8,12},{12,8},{16,20},{20,16},{24,28},{28,24},{1,5},{5... | collective-permute-start | bytes 393224 | tf_op jit(solution)/shard_map/ppermute | solution.py:58
  68.6 14.2 %collective-permute-start.32 = (bf16[32,2048]{1,0:T(8,128)(2,1)S(1)}, bf16[32,2048]{1,0:T(8,128)(2,1)S(1)}, u32[]{:S(2)}, u32[]{:S(2)}) collective-permute-start(bf16[32,2048]{1,0:T(8,128)(2,1)S(1)} %get-tuple-element.81), channel_id=1, source_target_pairs={{0,8},{4,12},{8,0},{12,4},{16,24},{20,28},{24,16},{28,20},{1,9},{5... | collective-permute-start | bytes 393224 | tf_op jit(solution)/shard_map/ppermute | solution.py:58
  72.1 11.1 %collective-permute-start.33 = (bf16[32,2048]{1,0:T(8,128)(2,1)S(1)}, bf16[32,2048]{1,0:T(8,128)(2,1)S(1)}, u32[]{:S(2)}, u32[]{:S(2)}) collective-permute-start(bf16[32,2048]{1,0:T(8,128)(2,1)S(1)} %get-tuple-element.82), channel_id=1, source_target_pairs={{0,12},{4,8},{8,4},{12,0},{16,28},{20,24},{24,20},{28,16},{1,13},{... | collective-permute-start | bytes 393224 | tf_op jit(solution)/shard_map/ppermute | solution.py:58
  72.8 54.0 %collective-permute-start.36 = (bf16[768,512]{1,0:T(8,128)(2,1)S(1)}, bf16[768,512]{1,0:T(8,128)(2,1)S(1)}, u32[]{:S(2)}, u32[]{:S(2)}) collective-permute-start(bf16[768,512]{1,0:T(8,128)(2,1)S(1)} %shard_map.104), channel_id=1, source_target_pairs={{0,2},{1,3},{2,0},{3,1},{4,6},{5,7},{6,4},{7,5},{8,10},{9,11},{10,... | collective-permute-start | bytes 2359304 | tf_op jit(solution)/shard_map/ppermute | solution.py:58
  83.6 29.5 %collective-permute-start.34 = (bf16[96,2048]{1,0:T(8,128)(2,1)S(1)}, bf16[96,2048]{1,0:T(8,128)(2,1)S(1)}, u32[]{:S(2)}, u32[]{:S(2)}) collective-permute-start(bf16[96,2048]{1,0:T(8,128)(2,1)S(1)} %shard_map.100), channel_id=1, source_target_pairs={{0,16},{4,20},{8,24},{12,28},{16,0},{20,4},{24,8},{28,12},{1,17},{... | collective-permute-start | bytes 1179656 | tf_op jit(solution)/shard_map/ppermute | solution.py:58
  85.3 10.2 %collective-permute-start.28 = (bf16[32,2048]{1,0:T(8,128)(2,1)S(1)}, bf16[32,2048]{1,0:T(8,128)(2,1)S(1)}, u32[]{:S(2)}, u32[]{:S(2)}) collective-permute-start(bf16[32,2048]{1,0:T(8,128)(2,1)S(1)} %get-tuple-element.76), channel_id=1, source_target_pairs={{0,4},{4,0},{8,12},{12,8},{16,20},{20,16},{24,28},{28,24},{1,5},{5... | collective-permute-start | bytes 393224 | tf_op jit(solution)/shard_map/ppermute | solution.py:58
  92.4 33.3 %collective-permute-start.20 = (bf16[96,2048]{1,0:T(8,128)(2,1)S(1)}, bf16[96,2048]{1,0:T(8,128)(2,1)S(1)}, u32[]{:S(2)}, u32[]{:S(2)}) collective-permute-start(bf16[96,2048]{1,0:T(8,128)(2,1)S(1)} %shard_map.97), channel_id=1, source_target_pairs={{0,16},{4,20},{8,24},{12,28},{16,0},{20,4},{24,8},{28,12},{1,17},{... | collective-permute-start | bytes 1179656 | tf_op jit(solution)/shard_map/ppermute | solution.py:58
  92.8 15.8 %collective-permute-start.29 = (bf16[32,2048]{1,0:T(8,128)(2,1)S(1)}, bf16[32,2048]{1,0:T(8,128)(2,1)S(1)}, u32[]{:S(2)}, u32[]{:S(2)}) collective-permute-start(bf16[32,2048]{1,0:T(8,128)(2,1)S(1)} %get-tuple-element.77), channel_id=1, source_target_pairs={{0,8},{4,12},{8,0},{12,4},{16,24},{20,28},{24,16},{28,20},{1,9},{5... | collective-permute-start | bytes 393224 | tf_op jit(solution)/shard_map/ppermute | solution.py:58
  95.5 14.6 %collective-permute-start.30 = (bf16[32,2048]{1,0:T(8,128)(2,1)S(1)}, bf16[32,2048]{1,0:T(8,128)(2,1)S(1)}, u32[]{:S(2)}, u32[]{:S(2)}) collective-permute-start(bf16[32,2048]{1,0:T(8,128)(2,1)S(1)} %get-tuple-element.78), channel_id=1, source_target_pairs={{0,12},{4,8},{8,4},{12,0},{16,28},{20,24},{24,20},{28,16},{1,13},{... | collective-permute-start | bytes 393224 | tf_op jit(solution)/shard_map/ppermute | solution.py:58
  110.1 12.4 %collective-permute-start.14 = (bf16[32,2048]{1,0:T(8,128)(2,1)S(1)}, bf16[32,2048]{1,0:T(8,128)(2,1)S(1)}, u32[]{:S(2)}, u32[]{:S(2)}) collective-permute-start(bf16[32,2048]{1,0:T(8,128)(2,1)S(1)} %get-tuple-element.61), channel_id=1, source_target_pairs={{0,8},{4,12},{8,0},{12,4},{16,24},{20,28},{24,16},{28,20},{1,9},{5... | collective-permute-start | bytes 393224 | tf_op jit(solution)/shard_map/ppermute | solution.py:58
  113.0 12.7 %collective-permute-start.15 = (bf16[32,2048]{1,0:T(8,128)(2,1)S(1)}, bf16[32,2048]{1,0:T(8,128)(2,1)S(1)}, u32[]{:S(2)}, u32[]{:S(2)}) collective-permute-start(bf16[32,2048]{1,0:T(8,128)(2,1)S(1)} %get-tuple-element.62), channel_id=1, source_target_pairs={{0,12},{4,8},{8,4},{12,0},{16,28},{20,24},{24,20},{28,16},{1,13},{... | collective-permute-start | bytes 393224 | tf_op jit(solution)/shard_map/ppermute | solution.py:58
  (20 other events, 187.3 us)

commit v3 on v2

--- a/solution.py
+++ b/solution.py
@@ -68,6 +68,7 @@
 
 STEP = 512
 RELAYED = (0, 1)
+CUTS = 2
 
 
 def row_tables(refs, b, peer_slots, relative):
@@ -211,18 +212,21 @@
     )
 
 
-def collect_rows(blocks, tables, b, peers, peer_slots, relative, last=False, extras=(), previous=None):
+def collect_rows(blocks, tables, b, peers, peer_slots, relative, parts=1, last=False, extras=(), previous=None):
     width = blocks[0].shape[1]
     micro_count, rows = tables[0].shape
+    if len(tables) == 1:
+        micro_count //= 2
     count = len(blocks)
     ahead = len(tables)
     block_rows = blocks[0].shape[0]
     slot_count = peers * peer_slots
+    part_width = width // parts
 
     def body(*refs):
         block_refs = refs[ahead : ahead + count]
         extra_refs = refs[ahead + count : ahead + count + len(extras)]
-        out_ref, stage = refs[-2:]
+        out_refs, stage = refs[-1 - parts : -1], refs[-1]
         position = as_column(row_tables(refs[:ahead], b, peer_slots, relative)[1])
         slot_ids = lax.broadcasted_iota(jnp.int32, (rows, slot_count), 1)
         taking = jnp.where(slot_ids == position, 1.0, 0.0).astype(BF16)
@@ -231,16 +235,19 @@
         for start in range(0, width, STEP):
             columns = slice(start, start + STEP)
             taken = jnp.dot(taking, stage[:, columns], preferred_element_type=F32)
-            for ref in extra_refs:
-                taken = taken + ref[:, columns].astype(F32)
+            if extras:
+                extra_width = width // len(extras)
+                offset = start % extra_width
+                taken = taken + extra_refs[start // extra_width][:, offset : offset + STEP].astype(F32)
             if last:
-                out_ref[0, :, columns] = taken.astype(BF16)
+                out_refs[0][0, :, columns] = taken.astype(BF16)
             else:
-                out_ref[:, columns] = taken.astype(BF16)
+                offset = start % part_width
+                out_refs[start // part_width][:, offset : offset + STEP] = taken.astype(BF16)
 
     operands = [*tables, *blocks, *extras]
     in_specs = [resident_spec()] * len(operands)
-    out_shape, out_specs, aliases = (rows, width), None, {}
+    out_shape, out_specs, aliases = (rows, part_width), None, {}
     if last:
         out_shape = (micro_count, rows, width)
         out_specs = [pl.BlockSpec((1, rows, width), lambda i: (b, 0, 0))]
@@ -251,13 +258,13 @@
     return call(
         body,
         operands,
-        [(out_shape, BF16)],
+        [(out_shape, BF16)] * parts,
         flops=2 * slot_count * rows * width,
         in_specs=in_specs,
         out_specs=out_specs,
         scratch=[pltpu.VMEM((slot_count, width), BF16)],
         aliases=aliases,
-    )[0]
+    )
 
 
 def weight_parts(saved, grads, hidden, slots):
@@ -363,7 +370,7 @@
     for b in micros:
         blocks = place_rows(grads, tables, b, n_expert, peer_slots, relay)
         if relay:
-            turns = order if b == 0 else [*range(half, n_expert), *range(half - 1, 0, -1)]
+            turns = order if b == 0 else [1, 4, 5, 6, 7, 2, 3]
             moved = {k: send(blocks[k], k) for k in turns}
             arrived.append([blocks[0]] + [moved[k] for k in range(1, n_expert)])
         else:
@@ -392,10 +399,13 @@
         else:
             handed = [blocks[half]] + [send(blocks[half + k], k) for k in range(1, half)]
             near = [blocks[0]] + [send(blocks[k], k) for k in range(1, half)]
-            others = collect_rows(handed, far_tables, b, half, peer_slots, True)
-            extras = [send(others, half)]
+            parts = CUTS if b + 1 < micro_count else 1
+            others = collect_rows(handed, far_tables, b, half, peer_slots, True, parts)
+            extras = [send(others[i], half) for i in range(parts)]
             peers = half
-        in_rows = collect_rows(near, tables, b, peers, peer_slots, relay, True, extras, in_rows)
+        in_rows = collect_rows(
+            near, tables, b, peers, peer_slots, relay, 1, True, extras, in_rows
+        )[0]
     near, ours = weight_parts(saved, gu_all, hidden_all, slot_all)
     got_near = swap(near, "mirror", 1)
     pair = near_sum(ours, got_near)

time: 128 us -> 134 us (1.047)
  waiting for transfers between devices: 48.9 us -> 54.2 us
    ppermute x37 -> x38, waiting for transfers between devices: 48.9 us -> 54.2 us  [swap(): return lax.ppermute(value, axis, [(i, i ^ bit) for i in range(size)])]
    ppermute x37 -> x38, starting transfers between devices: 62.9 us -> 63.2 us  [swap(): return lax.ppermute(value, axis, [(i, i ^ bit) for i in range(size)])]
  transfers between devices with their start and end apart: 37 -> 38, of which waited for: 15 -> 16; matrix products, arithmetic and copies ran while one was open for 0% -> 0% of each run, Pallas kernels for 7% -> 7%
where the time goes in v3:
time: 134 us
  starting transfers between devices  63.2 us (47%)
  waiting for transfers between devices  54.2 us (40%)
  Pallas kernels  13.7 us (10%)
  local copies, waits for them, and re-layouts  1.62 us (1%)
    ppermute x38, starting transfers between devices, swap(): return lax.ppermute(value, axis, [(i, i ^ bit) for i in range(size)])  63.2 us
    ppermute x38, waiting for transfers between devices, swap(): return lax.ppermute(value, axis, [(i, i ^ bit) for i in range(size)])  54.2 us
    pallas_call x12, Pallas kernels, call(): pl.pallas_call(body, grid=(steps,), in_specs=in_specs or [resident_spec()...  13.7 us
  transfers between devices with their start and end apart: 38, of which 16 were waited for; matrix products, arithmetic and copies ran while one was open for 0% of the time, Pallas kernels for 7%

profile of v3, /device:TPU:0, one launch (start us, length us, event | category | flops | bytes accessed | tf_op | source)
XLA Modules:
  0.0 133.5 jit_solution(14576244971684449125)
XLA Ops:
  0.7 3.0 %collective-permute-start.8 = (bf16[512,512]{1,0:T(8,128)(2,1)}, bf16[512,512]{1,0:T(8,128)(2,1)S(1)}, u32[]{:S(2)}, u32[]{:S(2)}) collective-permute-start(bf16[512,512]{1,0:T(8,128)(2,1)} %bitcast.14), channel_id=1, source_target_pairs={{0,2},{1,3},{2,0},{3,1},{4,6},{5,7},{6,4},{7,5},{8,10},{9,11},{10,... | collective-permute-start | bytes 1572872 | tf_op jit(solution)/shard_map/ppermute | solution.py:58
  8.7 2.6 %collective-permute-start.3 = (bf16[32,2048]{1,0:T(8,128)(2,1)S(1)}, bf16[32,2048]{1,0:T(8,128)(2,1)S(1)}, u32[]{:S(2)}, u32[]{:S(2)}) collective-permute-start(bf16[32,2048]{1,0:T(8,128)(2,1)S(1)} %get-tuple-element.54), channel_id=1, source_target_pairs={{0,16},{4,20},{8,24},{12,28},{16,0},{20,4},{24,8},{28,12},{1,17},{... | collective-permute-start | bytes 393224 | tf_op jit(solution)/shard_map/ppermute | solution.py:58
  11.3 3.0 %collective-permute-start.4 = (bf16[32,2048]{1,0:T(8,128)(2,1)S(1)}, bf16[32,2048]{1,0:T(8,128)(2,1)S(1)}, u32[]{:S(2)}, u32[]{:S(2)}) collective-permute-start(bf16[32,2048]{1,0:T(8,128)(2,1)S(1)} %get-tuple-element.55), channel_id=1, source_target_pairs={{0,20},{4,16},{8,28},{12,24},{16,4},{20,0},{24,12},{28,8},{1,21},{... | collective-permute-start | bytes 393224 | tf_op jit(solution)/shard_map/ppermute | solution.py:58
  14.2 2.3 %collective-permute-done.1.refs_2_ = bf16[32,2048]{1,0:T(8,128)(2,1)S(1)} collective-permute-done((bf16[32,2048]{1,0:T(8,128)(2,1)S(1)}, bf16[32,2048]{1,0:T(8,128)(2,1)S(1)}, u32[]{:S(2)}, u32[]{:S(2)}) %collective-permute-start.1) | collective-permute-done | bytes 131104 | tf_op jit(solution)/shard_map/ppermute | solution.py:58
  18.4 6.3 %collective-permute-start.5 = (bf16[32,2048]{1,0:T(8,128)(2,1)S(1)}, bf16[32,2048]{1,0:T(8,128)(2,1)S(1)}, u32[]{:S(2)}, u32[]{:S(2)}) collective-permute-start(bf16[32,2048]{1,0:T(8,128)(2,1)S(1)} %get-tuple-element.56), channel_id=1, source_target_pairs={{0,24},{4,28},{8,16},{12,20},{16,8},{20,12},{24,0},{28,4},{1,25},{... | collective-permute-start | bytes 393224 | tf_op jit(solution)/shard_map/ppermute | solution.py:58
  25.4 4.4 %collective-permute-start.6 = (bf16[32,2048]{1,0:T(8,128)(2,1)S(1)}, bf16[32,2048]{1,0:T(8,128)(2,1)S(1)}, u32[]{:S(2)}, u32[]{:S(2)}) collective-permute-start(bf16[32,2048]{1,0:T(8,128)(2,1)S(1)} %get-tuple-element.57), channel_id=1, source_target_pairs={{0,28},{4,24},{8,20},{12,16},{16,12},{20,8},{24,4},{28,0},{1,29},{... | collective-permute-start | bytes 393224 | tf_op jit(solution)/shard_map/ppermute | solution.py:58
  33.7 2.6 %collective-permute-done.21.refs_1_ = bf16[32,2048]{1,0:T(8,128)(2,1)S(1)} collective-permute-done((bf16[32,2048]{1,0:T(8,128)(2,1)S(1)}, bf16[32,2048]{1,0:T(8,128)(2,1)S(1)}, u32[]{:S(2)}, u32[]{:S(2)}) %collective-permute-start.21) | collective-permute-done | bytes 131104 | tf_op jit(solution)/shard_map/ppermute | solution.py:58
  37.9 3.5 %collective-permute-done.22.refs_2_ = bf16[32,2048]{1,0:T(8,128)(2,1)S(1)} collective-permute-done((bf16[32,2048]{1,0:T(8,128)(2,1)S(1)}, bf16[32,2048]{1,0:T(8,128)(2,1)S(1)}, u32[]{:S(2)}, u32[]{:S(2)}) %collective-permute-start.22) | collective-permute-done | bytes 131104 | tf_op jit(solution)/shard_map/ppermute | solution.py:58
  41.4 3.6 %collective-permute-start.23 = (bf16[32,2048]{1,0:T(8,128)(2,1)S(1)}, bf16[32,2048]{1,0:T(8,128)(2,1)S(1)}, u32[]{:S(2)}, u32[]{:S(2)}) collective-permute-start(bf16[32,2048]{1,0:T(8,128)(2,1)S(1)} %get-tuple-element.72), channel_id=1, source_target_pairs={{0,12},{4,8},{8,4},{12,0},{16,28},{20,24},{24,20},{28,16},{1,13},{... | collective-permute-start | bytes 393224 | tf_op jit(solution)/shard_map/ppermute | solution.py:58
  46.8 2.0 %collective-permute-start.26 = (bf16[32,2048]{1,0:T(8,128)(2,1)S(1)}, bf16[32,2048]{1,0:T(8,128)(2,1)S(1)}, u32[]{:S(2)}, u32[]{:S(2)}) collective-permute-start(bf16[32,2048]{1,0:T(8,128)(2,1)S(1)} %get-tuple-element.75), channel_id=1, source_target_pairs={{0,24},{4,28},{8,16},{12,20},{16,8},{20,12},{24,0},{28,4},{1,25},{... | collective-permute-start | bytes 393224 | tf_op jit(solution)/shard_map/ppermute | solution.py:58
  48.8 3.8 %collective-permute-start.27 = (bf16[32,2048]{1,0:T(8,128)(2,1)S(1)}, bf16[32,2048]{1,0:T(8,128)(2,1)S(1)}, u32[]{:S(2)}, u32[]{:S(2)}) collective-permute-start(bf16[32,2048]{1,0:T(8,128)(2,1)S(1)} %get-tuple-element.76), channel_id=1, source_target_pairs={{0,28},{4,24},{8,20},{12,16},{16,12},{20,8},{24,4},{28,0},{1,29},{... | collective-permute-start | bytes 393224 | tf_op jit(solution)/shard_map/ppermute | solution.py:58
  57.3 3.2 %collective-permute-done.24.refs_4_ = bf16[32,2048]{1,0:T(8,128)(2,1)S(1)} collective-permute-done((bf16[32,2048]{1,0:T(8,128)(2,1)S(1)}, bf16[32,2048]{1,0:T(8,128)(2,1)S(1)}, u32[]{:S(2)}, u32[]{:S(2)}) %collective-permute-start.24) | collective-permute-done | bytes 131104 | tf_op jit(solution)/shard_map/ppermute | solution.py:58
  60.6 2.5 %collective-permute-done.25.refs_5_ = bf16[32,2048]{1,0:T(8,128)(2,1)S(1)} collective-permute-done((bf16[32,2048]{1,0:T(8,128)(2,1)S(1)}, bf16[32,2048]{1,0:T(8,128)(2,1)S(1)}, u32[]{:S(2)}, u32[]{:S(2)}) %collective-permute-start.25) | collective-permute-done | bytes 131104 | tf_op jit(solution)/shard_map/ppermute | solution.py:58
  71.8 3.8 %collective-permute-start.18 = (bf16[32,2048]{1,0:T(8,128)(2,1)S(1)}, bf16[32,2048]{1,0:T(8,128)(2,1)S(1)}, u32[]{:S(2)}, u32[]{:S(2)}) collective-permute-start(bf16[32,2048]{1,0:T(8,128)(2,1)S(1)} %get-tuple-element.67), channel_id=1, source_target_pairs={{0,8},{4,12},{8,0},{12,4},{16,24},{20,28},{24,16},{28,20},{1,9},{5... | collective-permute-start | bytes 393224 | tf_op jit(solution)/shard_map/ppermute | solution.py:58
  75.8 3.2 %collective-permute-start.16 = (f32[4,96]{1,0:T(4,128)S(1)}, f32[4,96]{1,0:T(4,128)S(1)}, u32[]{:S(2)}, u32[]{:S(2)}) collective-permute-start(f32[4,96]{1,0:T(4,128)S(1)} %pad_maximum_fusion), channel_id=1, source_target_pairs={{0,16},{4,20},{8,24},{12,28},{16,0},{20,4},{24,8},{28,12},{1,17},{... | collective-permute-start | bytes 4616 | tf_op jit(solution)/shard_map/ppermute | solution.py:58
  79.0 2.2 %collective-permute-done.16.refs_0_ = f32[4,96]{1,0:T(4,128)S(1)} collective-permute-done((f32[4,96]{1,0:T(4,128)S(1)}, f32[4,96]{1,0:T(4,128)S(1)}, u32[]{:S(2)}, u32[]{:S(2)}) %collective-permute-start.16) | collective-permute-done | bytes 1568 | tf_op jit(solution)/shard_map/ppermute | solution.py:58
  82.0 3.7 %collective-permute-start.32 = (bf16[32,2048]{1,0:T(8,128)(2,1)S(1)}, bf16[32,2048]{1,0:T(8,128)(2,1)S(1)}, u32[]{:S(2)}, u32[]{:S(2)}) collective-permute-start(bf16[32,2048]{1,0:T(8,128)(2,1)S(1)} %get-tuple-element.83), channel_id=1, source_target_pairs={{0,8},{4,12},{8,0},{12,4},{16,24},{20,28},{24,16},{28,20},{1,9},{5... | collective-permute-start | bytes 393224 | tf_op jit(solution)/shard_map/ppermute | solution.py:58
  87.2 4.5 %collective-permute-start.29 = (bf16[32,2048]{1,0:T(8,128)(2,1)S(1)}, bf16[32,2048]{1,0:T(8,128)(2,1)S(1)}, u32[]{:S(2)}, u32[]{:S(2)}) collective-permute-start(bf16[32,2048]{1,0:T(8,128)(2,1)S(1)} %get-tuple-element.79), channel_id=1, source_target_pairs={{0,8},{4,12},{8,0},{12,4},{16,24},{20,28},{24,16},{28,20},{1,9},{5... | collective-permute-start | bytes 393224 | tf_op jit(solution)/shard_map/ppermute | solution.py:58
  92.2 3.3 %collective-permute-done.33.refs_4_ = bf16[32,2048]{1,0:T(8,128)(2,1)S(1)} collective-permute-done((bf16[32,2048]{1,0:T(8,128)(2,1)S(1)}, bf16[32,2048]{1,0:T(8,128)(2,1)S(1)}, u32[]{:S(2)}, u32[]{:S(2)}) %collective-permute-start.33) | collective-permute-done | bytes 131104 | tf_op jit(solution)/shard_map/ppermute | solution.py:58
  95.9 2.9 %collective-permute-start.35 = (bf16[96,1024]{1,0:T(8,128)(2,1)S(1)}, bf16[96,1024]{1,0:T(8,128)(2,1)S(1)}, u32[]{:S(2)}, u32[]{:S(2)}) collective-permute-start(bf16[96,1024]{1,0:T(8,128)(2,1)S(1)} %get-tuple-element.86), channel_id=1, source_target_pairs={{0,16},{4,20},{8,24},{12,28},{16,0},{20,4},{24,8},{28,12},{1,17},{... | collective-permute-start | bytes 589832 | tf_op jit(solution)/shard_map/ppermute | solution.py:58
  99.1 13.6 %collective-permute-done.30.refs_6_ = bf16[32,2048]{1,0:T(8,128)(2,1)S(1)} collective-permute-done((bf16[32,2048]{1,0:T(8,128)(2,1)S(1)}, bf16[32,2048]{1,0:T(8,128)(2,1)S(1)}, u32[]{:S(2)}, u32[]{:S(2)}) %collective-permute-start.30) | collective-permute-done | bytes 131104 | tf_op jit(solution)/shard_map/ppermute | solution.py:58
  113.8 9.5 %collective-permute-done.34.refs_7_ = bf16[96,1024]{1,0:T(8,128)(2,1)S(1)} collective-permute-done((bf16[96,1024]{1,0:T(8,128)(2,1)S(1)}, bf16[96,1024]{1,0:T(8,128)(2,1)S(1)}, u32[]{:S(2)}, u32[]{:S(2)}) %collective-permute-start.34) | collective-permute-done | bytes 196640 | tf_op jit(solution)/shard_map/ppermute | solution.py:58
  123.3 2.1 %collective-permute-done.35.refs_8_ = bf16[96,1024]{1,0:T(8,128)(2,1)S(1)} collective-permute-done((bf16[96,1024]{1,0:T(8,128)(2,1)S(1)}, bf16[96,1024]{1,0:T(8,128)(2,1)S(1)}, u32[]{:S(2)}, u32[]{:S(2)}) %collective-permute-start.35) | collective-permute-done | bytes 196640 | tf_op jit(solution)/shard_map/ppermute | solution.py:58
  126.8 2.7 %collective-permute-done.14.refs_5_ = bf16[32,2048]{1,0:T(8,128)(2,1)S(1)} collective-permute-done((bf16[32,2048]{1,0:T(8,128)(2,1)S(1)}, bf16[32,2048]{1,0:T(8,128)(2,1)S(1)}, u32[]{:S(2)}, u32[]{:S(2)}) %collective-permute-start.14) | collective-permute-done | bytes 131104 | tf_op jit(solution)/shard_map/ppermute | solution.py:58
  (80 shorter events, 38.4 us)
Async XLA Ops:
  0.7 17.7 %collective-permute-start.8 = (bf16[512,512]{1,0:T(8,128)(2,1)}, bf16[512,512]{1,0:T(8,128)(2,1)S(1)}, u32[]{:S(2)}, u32[]{:S(2)}) collective-permute-start(bf16[512,512]{1,0:T(8,128)(2,1)} %bitcast.14), channel_id=1, source_target_pairs={{0,2},{1,3},{2,0},{3,1},{4,6},{5,7},{6,4},{7,5},{8,10},{9,11},{10,... | collective-permute-start | bytes 1572872 | tf_op jit(solution)/shard_map/ppermute | solution.py:58
  11.3 14.1 %collective-permute-start.4 = (bf16[32,2048]{1,0:T(8,128)(2,1)S(1)}, bf16[32,2048]{1,0:T(8,128)(2,1)S(1)}, u32[]{:S(2)}, u32[]{:S(2)}) collective-permute-start(bf16[32,2048]{1,0:T(8,128)(2,1)S(1)} %get-tuple-element.55), channel_id=1, source_target_pairs={{0,20},{4,16},{8,28},{12,24},{16,4},{20,0},{24,12},{28,8},{1,21},{... | collective-permute-start | bytes 393224 | tf_op jit(solution)/shard_map/ppermute | solution.py:58
  16.6 28.4 %collective-permute-start.7 = (bf16[512,512]{1,0:T(8,128)(2,1)}, bf16[512,512]{1,0:T(8,128)(2,1)S(1)}, u32[]{:S(2)}, u32[]{:S(2)}) collective-permute-start(bf16[512,512]{1,0:T(8,128)(2,1)} %bitcast.15), channel_id=1, source_target_pairs={{0,1},{1,0},{2,3},{3,2},{4,5},{5,4},{6,7},{7,6},{8,9},{9,8},{10,11... | collective-permute-start | bytes 1572872 | tf_op jit(solution)/shard_map/ppermute | solution.py:58
  18.3 14.9 %collective-permute-start.11 = (bf16[64,2048]{1,0:T(8,128)(2,1)}, bf16[64,2048]{1,0:T(8,128)(2,1)S(1)}, u32[]{:S(2)}, u32[]{:S(2)}) collective-permute-start(bf16[64,2048]{1,0:T(8,128)(2,1)} %bitcast.17), channel_id=1, source_target_pairs={{0,2},{1,3},{2,0},{3,1},{4,6},{5,7},{6,4},{7,5},{8,10},{9,11},{10,... | collective-permute-start | bytes 786440 | tf_op jit(solution)/shard_map/ppermute | solution.py:58
  18.4 30.5 %collective-permute-start.9 = (bf16[512,512]{1,0:T(8,128)(2,1)S(1)}, bf16[512,512]{1,0:T(8,128)(2,1)S(1)}, u32[]{:S(2)}, u32[]{:S(2)}) collective-permute-start(bf16[512,512]{1,0:T(8,128)(2,1)S(1)} %collective-permute-done.8.refs_2_), channel_id=1, source_target_pairs={{0,1},{1,0},{2,3},{3,2},{4,5},{5,4},{6,7},{7,6},{8,9},{9,8},{10,11... | collective-permute-start | bytes 1572872 | tf_op jit(solution)/shard_map/ppermute | solution.py:58
  18.4 12.9 %collective-permute-start.5 = (bf16[32,2048]{1,0:T(8,128)(2,1)S(1)}, bf16[32,2048]{1,0:T(8,128)(2,1)S(1)}, u32[]{:S(2)}, u32[]{:S(2)}) collective-permute-start(bf16[32,2048]{1,0:T(8,128)(2,1)S(1)} %get-tuple-element.56), channel_id=1, source_target_pairs={{0,24},{4,28},{8,16},{12,20},{16,8},{20,12},{24,0},{28,4},{1,25},{... | collective-permute-start | bytes 393224 | tf_op jit(solution)/shard_map/ppermute | solution.py:58
  33.2 11.8 %collective-permute-start.10 = (bf16[64,2048]{1,0:T(8,128)(2,1)S(1)}, bf16[64,2048]{1,0:T(8,128)(2,1)S(1)}, u32[]{:S(2)}, u32[]{:S(2)}) collective-permute-start(bf16[64,2048]{1,0:T(8,128)(2,1)S(1)} %bitcast.18), channel_id=1, source_target_pairs={{0,1},{1,0},{2,3},{3,2},{4,5},{5,4},{6,7},{7,6},{8,9},{9,8},{10,11... | collective-permute-start | bytes 786440 | tf_op jit(solution)/shard_map/ppermute | solution.py:58
  33.2 13.6 %collective-permute-start.12 = (bf16[64,2048]{1,0:T(8,128)(2,1)S(1)}, bf16[64,2048]{1,0:T(8,128)(2,1)S(1)}, u32[]{:S(2)}, u32[]{:S(2)}) collective-permute-start(bf16[64,2048]{1,0:T(8,128)(2,1)S(1)} %collective-permute-done.11.refs_6_), channel_id=1, source_target_pairs={{0,1},{1,0},{2,3},{3,2},{4,5},{5,4},{6,7},{7,6},{8,9},{9,8},{10,11... | collective-permute-start | bytes 786440 | tf_op jit(solution)/shard_map/ppermute | solution.py:58
  41.4 15.9 %collective-permute-start.23 = (bf16[32,2048]{1,0:T(8,128)(2,1)S(1)}, bf16[32,2048]{1,0:T(8,128)(2,1)S(1)}, u32[]{:S(2)}, u32[]{:S(2)}) collective-permute-start(bf16[32,2048]{1,0:T(8,128)(2,1)S(1)} %get-tuple-element.72), channel_id=1, source_target_pairs={{0,12},{4,8},{8,4},{12,0},{16,28},{20,24},{24,20},{28,16},{1,13},{... | collective-permute-start | bytes 393224 | tf_op jit(solution)/shard_map/ppermute | solution.py:58
  44.9 15.6 %collective-permute-start.24 = (bf16[32,2048]{1,0:T(8,128)(2,1)S(1)}, bf16[32,2048]{1,0:T(8,128)(2,1)S(1)}, u32[]{:S(2)}, u32[]{:S(2)}) collective-permute-start(bf16[32,2048]{1,0:T(8,128)(2,1)S(1)} %get-tuple-element.73), channel_id=1, source_target_pairs={{0,16},{4,20},{8,24},{12,28},{16,0},{20,4},{24,8},{28,12},{1,17},{... | collective-permute-start | bytes 393224 | tf_op jit(solution)/shard_map/ppermute | solution.py:58
  45.0 18.1 %collective-permute-start.25 = (bf16[32,2048]{1,0:T(8,128)(2,1)S(1)}, bf16[32,2048]{1,0:T(8,128)(2,1)S(1)}, u32[]{:S(2)}, u32[]{:S(2)}) collective-permute-start(bf16[32,2048]{1,0:T(8,128)(2,1)S(1)} %get-tuple-element.74), channel_id=1, source_target_pairs={{0,20},{4,16},{8,28},{12,24},{16,4},{20,0},{24,12},{28,8},{1,21},{... | collective-permute-start | bytes 393224 | tf_op jit(solution)/shard_map/ppermute | solution.py:58
  46.8 16.3 %collective-permute-start.26 = (bf16[32,2048]{1,0:T(8,128)(2,1)S(1)}, bf16[32,2048]{1,0:T(8,128)(2,1)S(1)}, u32[]{:S(2)}, u32[]{:S(2)}) collective-permute-start(bf16[32,2048]{1,0:T(8,128)(2,1)S(1)} %get-tuple-element.75), channel_id=1, source_target_pairs={{0,24},{4,28},{8,16},{12,20},{16,8},{20,12},{24,0},{28,4},{1,25},{... | collective-permute-start | bytes 393224 | tf_op jit(solution)/shard_map/ppermute | solution.py:58
  48.8 14.2 %collective-permute-start.27 = (bf16[32,2048]{1,0:T(8,128)(2,1)S(1)}, bf16[32,2048]{1,0:T(8,128)(2,1)S(1)}, u32[]{:S(2)}, u32[]{:S(2)}) collective-permute-start(bf16[32,2048]{1,0:T(8,128)(2,1)S(1)} %get-tuple-element.76), channel_id=1, source_target_pairs={{0,28},{4,24},{8,20},{12,16},{16,12},{20,8},{24,4},{28,0},{1,29},{... | collective-permute-start | bytes 393224 | tf_op jit(solution)/shard_map/ppermute | solution.py:58
  66.8 15.2 %collective-permute-start.17 = (bf16[32,2048]{1,0:T(8,128)(2,1)S(1)}, bf16[32,2048]{1,0:T(8,128)(2,1)S(1)}, u32[]{:S(2)}, u32[]{:S(2)}) collective-permute-start(bf16[32,2048]{1,0:T(8,128)(2,1)S(1)} %get-tuple-element.66), channel_id=1, source_target_pairs={{0,4},{4,0},{8,12},{12,8},{16,20},{20,16},{24,28},{28,24},{1,5},{5... | collective-permute-start | bytes 393224 | tf_op jit(solution)/shard_map/ppermute | solution.py:58
  70.4 62.1 %collective-permute-start.37 = (bf16[768,512]{1,0:T(8,128)(2,1)S(1)}, bf16[768,512]{1,0:T(8,128)(2,1)S(1)}, u32[]{:S(2)}, u32[]{:S(2)}) collective-permute-start(bf16[768,512]{1,0:T(8,128)(2,1)S(1)} %shard_map.104), channel_id=1, source_target_pairs={{0,2},{1,3},{2,0},{3,1},{4,6},{5,7},{6,4},{7,5},{8,10},{9,11},{10,... | collective-permute-start | bytes 2359304 | tf_op jit(solution)/shard_map/ppermute | solution.py:58
  71.8 13.9 %collective-permute-start.18 = (bf16[32,2048]{1,0:T(8,128)(2,1)S(1)}, bf16[32,2048]{1,0:T(8,128)(2,1)S(1)}, u32[]{:S(2)}, u32[]{:S(2)}) collective-permute-start(bf16[32,2048]{1,0:T(8,128)(2,1)S(1)} %get-tuple-element.67), channel_id=1, source_target_pairs={{0,8},{4,12},{8,0},{12,4},{16,24},{20,28},{24,16},{28,20},{1,9},{5... | collective-permute-start | bytes 393224 | tf_op jit(solution)/shard_map/ppermute | solution.py:58
  75.6 10.7 %collective-permute-start.19 = (bf16[32,2048]{1,0:T(8,128)(2,1)S(1)}, bf16[32,2048]{1,0:T(8,128)(2,1)S(1)}, u32[]{:S(2)}, u32[]{:S(2)}) collective-permute-start(bf16[32,2048]{1,0:T(8,128)(2,1)S(1)} %get-tuple-element.68), channel_id=1, source_target_pairs={{0,12},{4,8},{8,4},{12,0},{16,28},{20,24},{24,20},{28,16},{1,13},{... | collective-permute-start | bytes 393224 | tf_op jit(solution)/shard_map/ppermute | solution.py:58
  82.0 10.1 %collective-permute-start.32 = (bf16[32,2048]{1,0:T(8,128)(2,1)S(1)}, bf16[32,2048]{1,0:T(8,128)(2,1)S(1)}, u32[]{:S(2)}, u32[]{:S(2)}) collective-permute-start(bf16[32,2048]{1,0:T(8,128)(2,1)S(1)} %get-tuple-element.83), channel_id=1, source_target_pairs={{0,8},{4,12},{8,0},{12,4},{16,24},{20,28},{24,16},{28,20},{1,9},{5... | collective-permute-start | bytes 393224 | tf_op jit(solution)/shard_map/ppermute | solution.py:58
  87.2 11.6 %collective-permute-start.29 = (bf16[32,2048]{1,0:T(8,128)(2,1)S(1)}, bf16[32,2048]{1,0:T(8,128)(2,1)S(1)}, u32[]{:S(2)}, u32[]{:S(2)}) collective-permute-start(bf16[32,2048]{1,0:T(8,128)(2,1)S(1)} %get-tuple-element.79), channel_id=1, source_target_pairs={{0,8},{4,12},{8,0},{12,4},{16,24},{20,28},{24,16},{28,20},{1,9},{5... | collective-permute-start | bytes 393224 | tf_op jit(solution)/shard_map/ppermute | solution.py:58
  92.1 39.2 %collective-permute-start.20 = (bf16[96,2048]{1,0:T(8,128)(2,1)S(1)}, bf16[96,2048]{1,0:T(8,128)(2,1)S(1)}, u32[]{:S(2)}, u32[]{:S(2)}) collective-permute-start(bf16[96,2048]{1,0:T(8,128)(2,1)S(1)} %shard_map.97), channel_id=1, source_target_pairs={{0,16},{4,20},{8,24},{12,28},{16,0},{20,4},{24,8},{28,12},{1,17},{... | collective-permute-start | bytes 1179656 | tf_op jit(solution)/shard_map/ppermute | solution.py:58
  95.8 27.5 %collective-permute-start.34 = (bf16[96,1024]{1,0:T(8,128)(2,1)S(1)}, bf16[96,1024]{1,0:T(8,128)(2,1)S(1)}, u32[]{:S(2)}, u32[]{:S(2)}) collective-permute-start(bf16[96,1024]{1,0:T(8,128)(2,1)S(1)} %get-tuple-element.85), channel_id=1, source_target_pairs={{0,16},{4,20},{8,24},{12,28},{16,0},{20,4},{24,8},{28,12},{1,17},{... | collective-permute-start | bytes 589832 | tf_op jit(solution)/shard_map/ppermute | solution.py:58
  95.9 29.5 %collective-permute-start.35 = (bf16[96,1024]{1,0:T(8,128)(2,1)S(1)}, bf16[96,1024]{1,0:T(8,128)(2,1)S(1)}, u32[]{:S(2)}, u32[]{:S(2)}) collective-permute-start(bf16[96,1024]{1,0:T(8,128)(2,1)S(1)} %get-tuple-element.86), channel_id=1, source_target_pairs={{0,16},{4,20},{8,24},{12,28},{16,0},{20,4},{24,8},{28,12},{1,17},{... | collective-permute-start | bytes 589832 | tf_op jit(solution)/shard_map/ppermute | solution.py:58
  98.8 13.9 %collective-permute-start.30 = (bf16[32,2048]{1,0:T(8,128)(2,1)S(1)}, bf16[32,2048]{1,0:T(8,128)(2,1)S(1)}, u32[]{:S(2)}, u32[]{:S(2)}) collective-permute-start(bf16[32,2048]{1,0:T(8,128)(2,1)S(1)} %get-tuple-element.80), channel_id=1, source_target_pairs={{0,12},{4,8},{8,4},{12,0},{16,28},{20,24},{24,20},{28,16},{1,13},{... | collective-permute-start | bytes 393224 | tf_op jit(solution)/shard_map/ppermute | solution.py:58
  112.7 14.1 %collective-permute-start.13 = (bf16[32,2048]{1,0:T(8,128)(2,1)S(1)}, bf16[32,2048]{1,0:T(8,128)(2,1)S(1)}, u32[]{:S(2)}, u32[]{:S(2)}) collective-permute-start(bf16[32,2048]{1,0:T(8,128)(2,1)S(1)} %get-tuple-element.62), channel_id=1, source_target_pairs={{0,4},{4,0},{8,12},{12,8},{16,20},{20,16},{24,28},{28,24},{1,5},{5... | collective-permute-start | bytes 393224 | tf_op jit(solution)/shard_map/ppermute | solution.py:58
  (21 other events, 196.5 us)
